TPU v7x, 32 devices: a whole 2x2x4 slice. The times are simulated.
32 devices in a mesh: dp: 4 (over y, core), fsdp: 8 (over z, x).
Axes of the slice: x: 2, y: 2, z: 4, core: 2. Of those that a mesh axis runs over, the one named last changes fastest.
Arguments:
- cells: bfloat16 [32768, 1024], P(('dp', 'fsdp')), may hold values from -6 to 6
- segment_ids: int32 [32, 1024], P(('dp', 'fsdp')), may hold values from 0 to 7, never falling along the last dimension, each value on 1 to 256 neighbouring positions
- valid: int32 [32, 1024], P(('dp', 'fsdp')), may hold values 0 or 1
- norm1_gain: bfloat16 [1024], P(('dp', 'fsdp')), may hold values from 0.5 to 1.5
- norm1_bias: bfloat16 [1024], P(('dp', 'fsdp')), may hold values from -3 to 3
- qkv_weight: bfloat16 [1024, 3072], P(('dp', 'fsdp')), may hold values from -0.1875 to 0.1875
- qv_bias: bfloat16 [2048], P(('dp', 'fsdp')), may hold values from -1 to 1
- out_weight: bfloat16 [1024, 1024], P(('dp', 'fsdp')), may hold values from -0.75 to 0.75
- out_bias: bfloat16 [1024], P(('dp', 'fsdp')), may hold values from -3 to 3
- norm2_gain: bfloat16 [1024], P(('dp', 'fsdp')), may hold values from 0.5 to 1.5
- norm2_bias: bfloat16 [1024], P(('dp', 'fsdp')), may hold values from -3 to 3
- up_weight: bfloat16 [1024, 4096], P(('dp', 'fsdp')), may hold values from -0.1875 to 0.1875
- up_bias: bfloat16 [4096], P(('dp', 'fsdp')), may hold values from -3 to 3
- down_weight: bfloat16 [4096, 1024], P(('dp', 'fsdp')), may hold values from -0.125 to 0.125
- down_bias: bfloat16 [1024], P(('dp', 'fsdp')), may hold values from -3 to 3
- out_grad: bfloat16 [32768, 1024], P(('dp', 'fsdp')), may hold values from -6 to 6
Outputs:
- out_cells: bfloat16 [32768, 1024], P(('dp', 'fsdp'))
- cells_grad: bfloat16 [32768, 1024], P(('dp', 'fsdp'))
- norm1_gain_grad: float32 [1024], P(('dp', 'fsdp'))
- norm1_bias_grad: float32 [1024], P(('dp', 'fsdp'))
- qkv_weight_grad: float32 [1024, 3072], P(('dp', 'fsdp'))
- qv_bias_grad: float32 [2048], P(('dp', 'fsdp'))
- out_weight_grad: float32 [1024, 1024], P(('dp', 'fsdp'))
- out_bias_grad: float32 [1024], P(('dp', 'fsdp'))
- norm2_gain_grad: float32 [1024], P(('dp', 'fsdp'))
- norm2_bias_grad: float32 [1024], P(('dp', 'fsdp'))
- up_weight_grad: float32 [1024, 4096], P(('dp', 'fsdp'))
- up_bias_grad: float32 [4096], P(('dp', 'fsdp'))
- down_weight_grad: float32 [4096, 1024], P(('dp', 'fsdp'))
- down_bias_grad: float32 [1024], P(('dp', 'fsdp'))
Inputs may be any that keep to these rules, and one draw needn't show every extreme that they name: `segment_ids`: along each row the slide numbers never fall; each slide covers 1 to 256 consecutive cells. `valid`: 1 marks a real cell, 0 padding, anywhere in a row.
All inputs are finite; a program needn't handle non-finite values. No bound on the sum of `valid` on one device may be relied on, other than what follows from the above.
Results may differ from a plain program's by a relative error of at most 0.013.
Values may be sent and summed in bfloat16 or wider, within the bound.
No kernel may reach another device: no remote copies, remote signals or barrier semaphores. Data moves between devices by JAX's collectives and lax.ppermute only.
A program may use at most 256 MiB of HBM per device.

v0:
```python
from functools import partial
import math

import jax
import jax.numpy as jnp
from jax import lax
from jax.sharding import PartitionSpec as P

HEADS = 16
HEAD = 64


EPSILON = 1e-05


def norm_rows(cell_rows, gain_vec, shift_vec):
    row_mean = jnp.mean(cell_rows, axis=-1, keepdims=True)
    centred = cell_rows - row_mean
    row_var = jnp.mean(centred * centred, axis=-1, keepdims=True)
    return centred * lax.rsqrt(row_var + EPSILON) * gain_vec + shift_vec


def norm_pull(cell_rows, gain_vec):
    zero_shift = jnp.zeros_like(gain_vec)
    normed_rows, pull_back = jax.vjp(norm_rows, cell_rows, gain_vec, zero_shift)
    return pull_back


def gelu_exact(values_in):
    return jax.nn.gelu(values_in, approximate=False)


def times_left(left_mat, right_mat):
    return lax.dot_general(
        left_mat, right_mat, (((0,), (0,)), ((), ())), preferred_element_type=jnp.float32
    )


def times_right(left_mat, right_mat):
    return lax.dot_general(
        left_mat, right_mat, (((1,), (1,)), ((), ())), preferred_element_type=jnp.float32
    )


def group_heads(tensor, num_groups):
    return tensor.reshape(tensor.shape[0], num_groups, -1).transpose(1, 0, 2)


def ungroup(tensor):
    return tensor.transpose(1, 0, 2).reshape(tensor.shape[1], -1)


def allowed_rows(slide_ids, live_keys, row_start, block_rows):
    num_rows = slide_ids.shape[0]
    row_places = row_start + jnp.arange(block_rows)
    col_places = jnp.arange(num_rows)
    same_slide = slide_ids[row_start : row_start + block_rows][:, None] == slide_ids[None, :]
    open_key = (live_keys[None, :] == 1) | (row_places[:, None] == col_places[None, :])
    return same_slide & open_key


def attend_forward(mask_blocks, block_rows, score_scale, group_item):
    query, key_rows, value_rows = group_item
    num_rows = query.shape[0]
    heads_here = query.shape[1] // HEAD
    query_heads = query.reshape(num_rows, heads_here, HEAD)
    key_heads = key_rows.reshape(num_rows, heads_here, HEAD)
    value_heads = value_rows.reshape(num_rows, heads_here, HEAD)
    out_parts = []
    lse_parts = []
    for block_id, row_start in enumerate(range(0, num_rows, block_rows)):
        scores = (
            jnp.einsum(
                "qhe,khe->hqk",
                query_heads[row_start : row_start + block_rows],
                key_heads,
                preferred_element_type=jnp.float32,
            )
            * score_scale
        )
        scores = jnp.where(mask_blocks[block_id][None], scores, -1e30)
        top_score = jnp.max(scores, axis=-1, keepdims=True)
        expd = jnp.exp(scores - top_score)
        row_total = jnp.sum(expd, axis=-1, keepdims=True)
        probs = (expd / row_total).astype(jnp.bfloat16)
        mixed = jnp.einsum("hqk,khe->qhe", probs, value_heads, preferred_element_type=jnp.float32)
        out_parts.append(mixed.astype(jnp.bfloat16).reshape(block_rows, -1))
        lse_parts.append((top_score + jnp.log(row_total))[..., 0])
    return (jnp.concatenate(out_parts, 0), jnp.concatenate(lse_parts, 1))


def attend_backward(mask_blocks, block_rows, score_scale, group_item):
    query, key_rows, value_rows, grad_rows, log_sums = group_item
    num_rows = query.shape[0]
    heads_here = query.shape[1] // HEAD
    query_heads = query.reshape(num_rows, heads_here, HEAD)
    key_heads = key_rows.reshape(num_rows, heads_here, HEAD)
    value_heads = value_rows.reshape(num_rows, heads_here, HEAD)
    grad_heads = grad_rows.reshape(num_rows, heads_here, HEAD)
    d_key_sum = jnp.zeros((num_rows, heads_here, HEAD), jnp.float32)
    d_value_sum = jnp.zeros((num_rows, heads_here, HEAD), jnp.float32)
    d_query_parts = []
    for block_id, row_start in enumerate(range(0, num_rows, block_rows)):
        query_block = query_heads[row_start : row_start + block_rows]
        grad_block = grad_heads[row_start : row_start + block_rows]
        scores = (
            jnp.einsum("qhe,khe->hqk", query_block, key_heads, preferred_element_type=jnp.float32)
            * score_scale
        )
        scores = jnp.where(mask_blocks[block_id][None], scores, -1e30)
        probs = jnp.exp(scores - log_sums[:, row_start : row_start + block_rows, None])
        d_value_sum = d_value_sum + jnp.einsum(
            "hqk,qhe->khe",
            probs.astype(jnp.bfloat16),
            grad_block,
            preferred_element_type=jnp.float32,
        )
        d_probs = jnp.einsum(
            "qhe,khe->hqk", grad_block, value_heads, preferred_element_type=jnp.float32
        )
        d_scores = (probs * (d_probs - jnp.sum(probs * d_probs, axis=-1, keepdims=True))).astype(
            jnp.bfloat16
        )
        d_query_block = (
            jnp.einsum("hqk,khe->qhe", d_scores, key_heads, preferred_element_type=jnp.float32)
            * score_scale
        )
        d_query_parts.append(d_query_block.astype(jnp.bfloat16).reshape(block_rows, -1))
        d_key_sum = d_key_sum + jnp.einsum(
            "hqk,qhe->khe", d_scores, query_block, preferred_element_type=jnp.float32
        )
    d_keys = (d_key_sum * score_scale).astype(jnp.bfloat16).reshape(num_rows, -1)
    d_values = d_value_sum.astype(jnp.bfloat16).reshape(num_rows, -1)
    return (jnp.concatenate(d_query_parts, 0), d_keys, d_values)


def local(
    cells,
    segment_ids,
    valid,
    norm1_gain,
    norm1_bias,
    qkv_weight,
    qv_bias,
    out_weight,
    out_bias,
    norm2_gain,
    norm2_bias,
    up_weight,
    up_bias,
    down_weight,
    down_bias,
    out_grad,
):
    num_rows, model_width = cells.shape
    block_rows = min(512, num_rows)
    score_scale = 1.0 / math.sqrt(HEAD)
    per_group = min(4, HEADS)
    num_groups = HEADS // per_group
    slide_ids = segment_ids[0]
    live_keys = valid[0]
    mask_blocks = [
        allowed_rows(slide_ids, live_keys, row_start, block_rows)
        for row_start in range(0, num_rows, block_rows)
    ]
    gain_one, shift_one, w_qkv, b_qv, w_out, b_out = (
        lax.all_gather(norm1_gain, ("dp", "fsdp"), axis=0, tiled=True),
        lax.all_gather(norm1_bias, ("dp", "fsdp"), axis=0, tiled=True),
        lax.all_gather(qkv_weight, ("dp", "fsdp"), axis=0, tiled=True),
        lax.all_gather(qv_bias, ("dp", "fsdp"), axis=0, tiled=True),
        lax.all_gather(out_weight, ("dp", "fsdp"), axis=0, tiled=True),
        lax.all_gather(out_bias, ("dp", "fsdp"), axis=0, tiled=True),
    )
    cell_rows = cells.astype(jnp.float32)
    normed = norm_rows(
        cell_rows, gain_one.astype(jnp.float32), shift_one.astype(jnp.float32)
    ).astype(jnp.bfloat16)
    qkv_all = jnp.dot(normed, w_qkv, preferred_element_type=jnp.float32)
    bias_float = b_qv.astype(jnp.float32)
    query = (qkv_all[:, :model_width] + bias_float[:model_width]).astype(jnp.bfloat16)
    key_rows = qkv_all[:, model_width : 2 * model_width].astype(jnp.bfloat16)
    value_rows = (qkv_all[:, 2 * model_width :] + bias_float[model_width:]).astype(jnp.bfloat16)
    query_groups = group_heads(query, num_groups)
    key_groups = group_heads(key_rows, num_groups)
    value_groups = group_heads(value_rows, num_groups)
    mixed_groups, lse_groups = lax.map(
        partial(attend_forward, mask_blocks, block_rows, score_scale),
        (query_groups, key_groups, value_groups),
    )
    mixed = ungroup(mixed_groups)
    inner = (
        cell_rows
        + jnp.dot(mixed, w_out, preferred_element_type=jnp.float32)
        + b_out.astype(jnp.float32)
    )
    gain_two, shift_two, w_up, b_up, w_down, b_down = (
        lax.all_gather(norm2_gain, ("dp", "fsdp"), axis=0, tiled=True),
        lax.all_gather(norm2_bias, ("dp", "fsdp"), axis=0, tiled=True),
        lax.all_gather(up_weight, ("dp", "fsdp"), axis=0, tiled=True),
        lax.all_gather(up_bias, ("dp", "fsdp"), axis=0, tiled=True),
        lax.all_gather(down_weight, ("dp", "fsdp"), axis=0, tiled=True),
        lax.all_gather(down_bias, ("dp", "fsdp"), axis=0, tiled=True),
    )
    normed_two = norm_rows(
        inner, gain_two.astype(jnp.float32), shift_two.astype(jnp.float32)
    ).astype(jnp.bfloat16)
    up_proj = jnp.dot(normed_two, w_up, preferred_element_type=jnp.float32) + b_up.astype(
        jnp.float32
    )
    hidden, gelu_back = jax.vjp(gelu_exact, up_proj)
    hidden_low = hidden.astype(jnp.bfloat16)
    layer_out = (
        inner
        + jnp.dot(hidden_low, w_down, preferred_element_type=jnp.float32)
        + b_down.astype(jnp.float32)
    )
    out_cells = layer_out.astype(jnp.bfloat16)
    gain_two_b, w_up_b, w_down_b = (
        lax.all_gather(norm2_gain, ("dp", "fsdp"), axis=0, tiled=True),
        lax.all_gather(up_weight, ("dp", "fsdp"), axis=0, tiled=True),
        lax.all_gather(down_weight, ("dp", "fsdp"), axis=0, tiled=True),
    )
    cot_rows = out_grad.astype(jnp.float32)
    d_down = times_left(hidden_low, out_grad)
    d_down_bias = jnp.sum(cot_rows, axis=0)
    d_hidden = times_right(out_grad, w_down_b)
    (d_up_full,) = gelu_back(d_hidden)
    d_up_low = d_up_full.astype(jnp.bfloat16)
    d_up_weight = times_left(normed_two, d_up_low)
    d_up_bias = jnp.sum(d_up_low.astype(jnp.float32), axis=0)
    d_normed_two = times_right(d_up_low, w_up_b)
    pull_two = norm_pull(inner, gain_two_b.astype(jnp.float32))
    d_inner_part, d_gain_two, d_shift_two = pull_two(d_normed_two)
    d_inner = cot_rows + d_inner_part
    ffn_grads = (
        lax.psum_scatter(d_gain_two, ("dp", "fsdp"), scatter_dimension=0, tiled=True),
        lax.psum_scatter(d_shift_two, ("dp", "fsdp"), scatter_dimension=0, tiled=True),
        lax.psum_scatter(d_up_weight, ("dp", "fsdp"), scatter_dimension=0, tiled=True),
        lax.psum_scatter(d_up_bias, ("dp", "fsdp"), scatter_dimension=0, tiled=True),
        lax.psum_scatter(d_down, ("dp", "fsdp"), scatter_dimension=0, tiled=True),
        lax.psum_scatter(d_down_bias, ("dp", "fsdp"), scatter_dimension=0, tiled=True),
    )
    gain_one_b, w_qkv_b, w_out_b = (
        lax.all_gather(norm1_gain, ("dp", "fsdp"), axis=0, tiled=True),
        lax.all_gather(qkv_weight, ("dp", "fsdp"), axis=0, tiled=True),
        lax.all_gather(out_weight, ("dp", "fsdp"), axis=0, tiled=True),
    )
    d_inner_low = d_inner.astype(jnp.bfloat16)
    d_out_weight = times_left(mixed, d_inner_low)
    d_out_bias = jnp.sum(d_inner_low.astype(jnp.float32), axis=0)
    d_mixed = times_right(d_inner_low, w_out_b).astype(jnp.bfloat16)
    d_query_g, d_key_g, d_value_g = lax.map(
        partial(attend_backward, mask_blocks, block_rows, score_scale),
        (query_groups, key_groups, value_groups, group_heads(d_mixed, num_groups), lse_groups),
    )
    d_query = ungroup(d_query_g)
    d_value = ungroup(d_value_g)
    d_qkv = jnp.concatenate([d_query, ungroup(d_key_g), d_value], axis=1)
    d_qkv_weight = times_left(normed, d_qkv)
    d_qv_bias = jnp.concatenate(
        [jnp.sum(d_query.astype(jnp.float32), axis=0), jnp.sum(d_value.astype(jnp.float32), axis=0)]
    )
    d_normed = times_right(d_qkv, w_qkv_b)
    pull_one = norm_pull(cell_rows, gain_one_b.astype(jnp.float32))
    d_rows_part, d_gain_one, d_shift_one = pull_one(d_normed)
    cells_grad = (d_inner + d_rows_part).astype(jnp.bfloat16)
    attn_grads = (
        lax.psum_scatter(d_gain_one, ("dp", "fsdp"), scatter_dimension=0, tiled=True),
        lax.psum_scatter(d_shift_one, ("dp", "fsdp"), scatter_dimension=0, tiled=True),
        lax.psum_scatter(d_qkv_weight, ("dp", "fsdp"), scatter_dimension=0, tiled=True),
        lax.psum_scatter(d_qv_bias, ("dp", "fsdp"), scatter_dimension=0, tiled=True),
        lax.psum_scatter(d_out_weight, ("dp", "fsdp"), scatter_dimension=0, tiled=True),
        lax.psum_scatter(d_out_bias, ("dp", "fsdp"), scatter_dimension=0, tiled=True),
    )
    return (
        out_cells,
        cells_grad,
        attn_grads[0],
        attn_grads[1],
        attn_grads[2],
        attn_grads[3],
        attn_grads[4],
        attn_grads[5],
        ffn_grads[0],
        ffn_grads[1],
        ffn_grads[2],
        ffn_grads[3],
        ffn_grads[4],
        ffn_grads[5],
    )


def solution(mesh):
    return jax.shard_map(
        local,
        mesh=mesh,
        in_specs=(
            P(("dp", "fsdp"), None),
            P(("dp", "fsdp"), None),
            P(("dp", "fsdp"), None),
            P(("dp", "fsdp")),
            P(("dp", "fsdp")),
            P(("dp", "fsdp"), None),
            P(("dp", "fsdp")),
            P(("dp", "fsdp"), None),
            P(("dp", "fsdp")),
            P(("dp", "fsdp")),
            P(("dp", "fsdp")),
            P(("dp", "fsdp"), None),
            P(("dp", "fsdp")),
            P(("dp", "fsdp"), None),
            P(("dp", "fsdp")),
            P(("dp", "fsdp"), None),
        ),
        out_specs=(
            P(("dp", "fsdp"), None),
            P(("dp", "fsdp"), None),
            P(("dp", "fsdp")),
            P(("dp", "fsdp")),
            P(("dp", "fsdp"), None),
            P(("dp", "fsdp")),
            P(("dp", "fsdp"), None),
            P(("dp", "fsdp")),
            P(("dp", "fsdp")),
            P(("dp", "fsdp")),
            P(("dp", "fsdp"), None),
            P(("dp", "fsdp")),
            P(("dp", "fsdp"), None),
            P(("dp", "fsdp")),
        ),
        check_vma=False,
    )
```

profile of v0, /device:TPU:0, one launch (start us, length us, event | category | flops | bytes accessed | tf_op | source)
XLA Modules:
  0.0 1437.7 jit_solution(5036215410979712915)
XLA Ops:
  15.9 42.6 %all-reduce.16 = (bf16[2048]{0:T(1024)(128)(2,1)S(1)}, bf16[1024]{0:T(1024)(128)(2,1)S(1)}, bf16[1024]{0:T(1024)(128)(2,1)S(1)}, bf16[1024]{0:T(1024)(128)(2,1)S...) all-reduce(bf16[2048]{0:T(1024)(128)(2,1)S(1)} %dynamic-update-slic, ...), channel_id=1, replica_groups=mesh['dp'=4,'fsdp'=8] {'dp','fsdp'}, use_global_device_ids=true, to_apply=%add.2 | all-reduce | flops 8192 | bytes 32768
  65.2 65.6 %all-gather = bf16[32,1,128]{2,1,0:T(2,128)(2,1)S(1)} all-gather(bf16[1,1,128]{2,1,0:T(2,128)(2,1)S(1)} %bitcast.254), channel_id=1, replica_groups=mesh['dp'=4,'fsdp'=8] {'dp','fsdp'}, dimensions={0}, use_global_device_ids=true | all-gather | bytes 8448 | tf_op jit(solution)/shard_map/all_gather | solution.py:200
  135.4 9.3 fusion.82
  161.8 77.0 %while.30 = (s32[]{:T(128)}, bf16[4,1024,256]{1,2,0:T(8,128)(2,1)}, f32[4,4,1024]{2,1,0:T(4,128)}, bf16[4,1024,256]{1,2,0:T(8,128)(2,1)}, bf16[4,1024,256]{1,2,0...) while((s32[]{:T(128)}, bf16[4,1024,256]{1,2,0:T(8,128)(2,1)}, ...), condition=%wide.region_7.8_spmd.clone.clone, body=%wide.region_2.7_spmd.clone.clone.sunk | while | flops 1129578496 | bytes 62041260 | solution.py:186
  238.8 7.5 fusion.92
  249.7 17.3 %fusion.85 = f32[1024,4096]{1,0:T(8,128)} fusion(bf16[1024,4096]{1,0:T(8,128)(2,1)} %all-gather.10.cloned.1.call-done, f32[1024,1024]{0,1:T(8,128)} %get-tuple-element.400, f32[1024]{0:T(1024)S(1)} %copy-done.55, f32[1024]{0:T(1024)S(1)} %copy-done.38, f32[1024]{0:T(1024)S(1)} %fusion.78, f32[1024]{0:T(1024)S(1)} %broadcast_multiply_fusion), kind=kOutput, calls=%fused_computation.154 | convolution fusion | flops 8595177472 | bytes 29376512 | tf_op jit(solution)/shard_map/dot_general | solution.py:207
  267.0 33.1 %all-gather.12.cloned.1.call-done = bf16[4096,1024]{1,0:T(8,128)(2,1)} async-done(((bf16[128,1024]{1,0:T(8,128)(2,1)}), bf16[4096,1024]{1,0:T(8,128)(2,1)}) %all-gather.12.cloned.1.call-update) | async-done | bytes 8388624 | tf_op jit(solution)/shard_map/all_gather | solution.py:201
  300.1 51.6 %convert_reduce_fusion = (f32[4096]{0:T(1024)}, bf16[1024,4096]{1,0:T(8,128)(2,1)S(1)}, f32[1024,4096]{1,0:T(8,128)}) fusion(f32[1024,4096]{1,0:T(8,128)} %fusion.85, f32[4096]{0:T(1024)S(1)} %bitcast.248, bf16[1024,1024]{1,0:T(8,128)(2,1)S(1)} %copy-done.13, bf16[4096,1024]{1,0:T(8,128)(2,1)} %all-gather.12.cloned.1.call-done), kind=kOutput, calls=%fused_computation.82 | convolution fusion | flops 8904503296 | bytes 52461568 | tf_op jit(solution)/shard_map/dot_general | solution.py:40
  351.7 11.2 fusion.94
  362.9 5.4 copy.48
  368.4 5.4 multiply_reduce_fusion.2
  384.9 5.2 convolution_convert_fusion
  395.1 145.4 %while.31 = (s32[]{:T(128)}, bf16[4,1024,256]{1,2,0:T(8,128)(2,1)}, bf16[4,1024,256]{1,2,0:T(8,128)(2,1)}, bf16[4,1024,256]{1,2,0:T(8,128)(2,1)}, bf16[4,1024,25...) while((s32[]{:T(128)}, bf16[4,1024,256]{1,2,0:T(8,128)(2,1)}, ...), condition=%wide.region_15.16_spmd.clone.clone, body=%wide.region_12.15_spmd.clone.clone.sunk | while | flops 2754342912 | bytes 148532432 | solution.py:252
  411.4 5.5 multiply_reduce_fusion.8
  416.9 4.7 multiply_convert_fusion.6
  447.6 5.5 multiply_reduce_fusion.8
  453.1 4.7 multiply_convert_fusion.6
  483.8 5.5 multiply_reduce_fusion.8
  489.2 4.7 multiply_convert_fusion.6
  520.0 5.5 multiply_reduce_fusion.8
  525.5 4.7 multiply_convert_fusion.6
  540.5 14.8 %fusion.74 = f32[1024,3072]{1,0:T(8,128)} fusion(bf16[1024,1024]{0,1:T(8,128)(2,1)} %bitcast.235, bf16[1024,1024]{0,1:T(8,128)(2,1)} %bitcast.240, bf16[1024,1024]{0,1:T(8,128)(2,1)} %bitcast.233, bf16[1024,1024]{0,1:T(8,128)(2,1)} %copy-done, f32[1024]{0:T(1024)S(1)} %copy-done.54, f32[1024]{0:T(1024)S(1)} %copy-done.30, f32[1024]{0:T(1024)S(1)} %copy-done.37, ...), kind=kOutput, calls=%fused_computation.133 | convolution fusion | flops 6467616768 | bytes 20987904 | tf_op jit(solution)/shard_map/dot_general | solution.py:34
  555.9 16.9 %fusion.84 = f32[1024,4096]{1,0:T(8,128)} fusion(bf16[1024,4096]{1,0:T(8,128)(2,1)} %copy-done.61, f32[1024,1024]{0,1:T(8,128)} %get-tuple-element.400, f32[1024]{0:T(1024)S(1)} %copy-done.56, f32[1024]{0:T(1024)S(1)} %copy-done.40, f32[1024]{0:T(1024)S(1)} %copy-done.43, f32[1024]{0:T(1024)S(1)} %copy-done.33), kind=kOutput, calls=%fused_computation.153 | convolution fusion | flops 8595177472 | bytes 29376512 | tf_op jit(solution)/shard_map/dot_general | solution.py:34
  573.6 14.2 multiply_convert_fusion.2
  591.2 11.5 fusion.99
  603.4 15.3 %add_convert_fusion.2 = bf16[1024,1024]{0,1:T(8,128)(2,1)} fusion(f32[1024,1024]{0,1:T(8,128)} %get-tuple-element.400, f32[1024]{0:T(1024)S(1)} %convert_element_type.144, bf16[1024,4096]{1,0:T(8,128)(2,1)} %copy-done.8, bf16[4096,1024]{1,0:T(8,128)(2,1)} %all-gather.12.cloned.1.call-done), kind=kOutput, calls=%fused_computation.129 | convolution fusion | flops 8593080320 | bytes 23072768 | tf_op jit(solution)/shard_map/dot_general | solution.py:214
  622.8 11.8 fusion.93
  634.6 5.7 copy.49
  656.3 41.1 %all-reduce.15 = (f32[1024]{0:T(1024)S(1)}, f32[1024]{0:T(1024)S(1)}, f32[2048]{0:T(1024)S(1)}, f32[1024]{0:T(1024)S(1)}, f32[1024]{0:T(1024)S(1)}, /*index=5*/f...) all-reduce(f32[1024]{0:T(1024)S(1)} %get-tuple-element.293, ...), channel_id=2, replica_groups=mesh['dp'=4,'fsdp'=8] {'dp','fsdp'}, use_global_device_ids=true, to_apply=%region_19.20.clone | all-reduce | flops 12288 | bytes 98304
  702.0 8.0 reduce-scatter.5.cloned.1.call-done
  710.0 360.2 %reduce-scatter.9.cloned.1.call-done = f32[32,4096]{1,0:T(8,128)} async-done(((f32[1024,4096]{1,0:T(8,128)}), f32[32,4096]{1,0:T(8,128)}) %reduce-scatter.9.cloned.1.call-update) | async-done | bytes 524304 | tf_op jit(solution)/shard_map/reduce_scatter | solution.py:238
  1070.2 360.3 %reduce-scatter.11.cloned.1.call-done = f32[128,1024]{1,0:T(8,128)} async-done(((f32[4096,1024]{1,0:T(8,128)}), f32[128,1024]{1,0:T(8,128)}) %reduce-scatter.11.cloned.1.call-update) | async-done | bytes 524304 | tf_op jit(solution)/shard_map/reduce_scatter | solution.py:240
  (340 shorter events, 266.4 us)
Async XLA Ops:
  7.2 128.2 %all-gather.6.cloned.1.call-start = ((), (), s32[]{:S(2)}) async-start(), calls=%async_computation.4 | async-start | bytes 6488064 | tf_op jit(solution)/shard_map/all_gather | solution.py:169
  7.9 230.9 %all-gather.8.cloned.1.call-start = ((), (), s32[]{:S(2)}) async-start(), calls=%async_computation.5 | async-start | bytes 2162688 | tf_op jit(solution)/shard_map/all_gather | solution.py:171
  8.7 241.0 %all-gather.10.cloned.1.call-start = ((), (), s32[]{:S(2)}) async-start(), calls=%async_computation.6 | async-start | bytes 8650752 | tf_op jit(solution)/shard_map/all_gather | solution.py:199
  9.4 290.7 %all-gather.12.cloned.1.call-start = ((), (), s32[]{:S(2)}) async-start(), calls=%async_computation.7 | async-start | bytes 8650752 | tf_op jit(solution)/shard_map/all_gather | solution.py:201
  10.0 692.0 %reduce-scatter.7.cloned.1.call-start = ((), (), s32[]{:S(2)}) async-start(), calls=%async_computation.9 | async-start | bytes 4325376 | tf_op jit(solution)/shard_map/reduce_scatter | solution.py:272
  62.3 82.4 %copy-start = (bf16[1024,1024]{0,1:T(8,128)(2,1)}, bf16[1024,1024]{0,1:T(8,128)(2,1)S(1)}, u32[]{:S(2)}) copy-start(bf16[1024,1024]{0,1:T(8,128)(2,1)S(1)} %copy.42) | copy-start | bytes 6291460
  62.3 73.0 %copy-start.53 = (f32[1024]{0:T(1024)}, f32[1024]{0:T(1024)S(1)}, u32[]{:S(2)}) copy-start(f32[1024]{0:T(1024)S(1)} %convert_element_type.133) | copy-start | bytes 12292
  62.3 73.0 %copy-start.29 = (f32[1024]{0:T(1024)}, f32[1024]{0:T(1024)S(1)}, u32[]{:S(2)}) copy-start(f32[1024]{0:T(1024)S(1)} %convert_element_type.132) | copy-start | bytes 12292
  62.7 82.0 %copy-start.25 = (f32[1024]{0:T(1024)}, f32[1024]{0:T(1024)S(1)}, u32[]{:S(2)}) copy-start(f32[1024]{0:T(1024)S(1)} %broadcast_multiply_fusion.1) | copy-start | bytes 12292
  63.4 81.3 %copy-start.36 = (f32[1024]{0:T(1024)}, f32[1024]{0:T(1024)S(1)}, u32[]{:S(2)}) copy-start(f32[1024]{0:T(1024)S(1)} %fusion.77) | copy-start | bytes 12292
  149.6 8.1 copy-start.9
  161.8 77.0 %copy-start.57 = (f32[1024]{0:T(1024)S(1)}, f32[1024]{0:T(1024)}, u32[]{:S(2)}) copy-start(f32[1024]{0:T(1024)} %convert_element_type.138) | copy-start | bytes 12292
  238.8 7.5 copy-start.17
  238.8 7.5 copy-start.19
  238.8 7.5 copy-start.21
  238.8 7.5 copy-start.23
  246.4 20.7 %copy-start.31 = (f32[1024]{0:T(1024)}, f32[1024]{0:T(1024)S(1)}, u32[]{:S(2)}) copy-start(f32[1024]{0:T(1024)S(1)} %broadcast_multiply_fusion) | copy-start | bytes 12292
  249.6 17.4 %copy-start.41 = (f32[1024]{0:T(1024)}, f32[1024]{0:T(1024)S(1)}, u32[]{:S(2)}) copy-start(f32[1024]{0:T(1024)S(1)} %fusion.78) | copy-start | bytes 12292
  249.6 50.5 %copy-start.13 = (bf16[1024,1024]{1,0:T(8,128)(2,1)S(1)}, bf16[1024,1024]{1,0:T(8,128)(2,1)}, u32[]{:S(2)}) copy-start(bf16[1024,1024]{1,0:T(8,128)(2,1)} %param.35) | copy-start | bytes 6291460
  249.6 50.5 %copy-start.27 = (f32[32,1,128]{2,1,0:T(1,128)S(1)}, f32[32,1,128]{2,1,0:T(1,128)}, u32[]{:S(2)}) copy-start(f32[32,1,128]{2,1,0:T(1,128)} %convert_element_type.155) | copy-start | bytes 49156
  300.1 51.6 %copy-start.60 = (bf16[1024,4096]{1,0:T(8,128)(2,1)S(1)}, bf16[1024,4096]{1,0:T(8,128)(2,1)}, u32[]{:S(2)}) copy-start(bf16[1024,4096]{1,0:T(8,128)(2,1)} %all-gather.10.cloned.1.call-done) | copy-start | bytes 25165828
  351.7 11.2 copy-start.61
  384.9 325.1 %reduce-scatter.5.cloned.1.call-start = ((), (), s32[]{:S(2)}) async-start(), calls=%async_computation.8 | async-start | bytes 12976128 | tf_op jit(solution)/shard_map/reduce_scatter | solution.py:270
  395.0 145.4 %copy-start.26 = (f32[1024]{0:T(1024)S(1)}, f32[1024]{0:T(1024)}, u32[]{:S(2)}) copy-start(f32[1024]{0:T(1024)} %copy-done.25) | copy-start | bytes 12292
  395.0 145.4 %copy-start.30 = (f32[1024]{0:T(1024)S(1)}, f32[1024]{0:T(1024)}, u32[]{:S(2)}) copy-start(f32[1024]{0:T(1024)} %copy-done.29) | copy-start | bytes 12292
  395.0 145.4 %copy-start.37 = (f32[1024]{0:T(1024)S(1)}, f32[1024]{0:T(1024)}, u32[]{:S(2)}) copy-start(f32[1024]{0:T(1024)} %copy-done.36) | copy-start | bytes 12292
  395.0 145.4 %copy-start.54 = (f32[1024]{0:T(1024)S(1)}, f32[1024]{0:T(1024)}, u32[]{:S(2)}) copy-start(f32[1024]{0:T(1024)} %copy-done.53) | copy-start | bytes 12292
  555.3 514.9 %reduce-scatter.9.cloned.1.call-start = ((), (), s32[]{:S(2)}) async-start(), calls=%async_computation.10 | async-start | bytes 17301504 | tf_op jit(solution)/shard_map/reduce_scatter | solution.py:238
  572.9 857.6 %reduce-scatter.11.cloned.1.call-start = ((), (), s32[]{:S(2)}) async-start(), calls=%async_computation.11 | async-start | bytes 17301504 | tf_op jit(solution)/shard_map/reduce_scatter | solution.py:240
  573.6 17.6 %copy-start.14 = (bf16[1024,1024]{1,0:T(8,128)(2,1)S(1)}, bf16[1024,1024]{1,0:T(8,128)(2,1)}, u32[]{:S(2)}) copy-start(bf16[1024,1024]{1,0:T(8,128)(2,1)} %param.35) | copy-start | bytes 6291460
  649.8 6.5 copy-start.50
  649.8 6.5 copy-start.51
  (38 other events, 135.4 us)
Sparse Core Ops, SparseCore 0:
  11.0 72.5 all-gather.5
  86.6 54.9 all-gather.7
  144.6 76.4 all-gather.9
  223.9 76.1 all-gather.11
  385.0 142.2 reduce-scatter.6
  555.4 154.5 reduce-scatter.4
  713.0 357.1 reduce-scatter.8
  1073.1 357.2 reduce-scatter.10
where the time goes:
time: 1450 us; the launch traced here: 1440 us
  waiting for transfers between devices  764 us (53%)
  matrix products  297 us (20%)
  blocking collectives  149 us (10%)
  other arithmetic  113 us (8%)
  local copies, waits for them, and re-layouts  97.7 us (7%)
  between operations  15.3 us (1%)
    reduce_scatter x1, waiting for transfers between devices, local(): lax.psum_scatter(d_down, ('dp', 'fsdp'), scatter_dimension=0, tiled=True)  360 us
    reduce_scatter x1, waiting for transfers between devices, local(): lax.psum_scatter(d_up_weight, ('dp', 'fsdp'), scatter_dimension=0, tiled=...  360 us
    unnamed x2, blocking collectives  83.6 us
    dot_general x4, matrix products, times_right(): lax.dot_general(left_mat, right_mat, (((1,), (1,)), ((), ())), preferred_...  79.8 us
    all_gather x1, blocking collectives, local(): lax.all_gather(up_bias, ('dp', 'fsdp'), axis=0, tiled=True)  65.6 us
    dot_general x4, matrix products, times_left(): lax.dot_general(left_mat, right_mat, (((0,), (0,)), ((), ())), preferred_...  47.7 us
    unnamed x152, local copies, waits for them, and re-layouts  35 us
    dot_general x8, matrix products, attend_backward(): jnp.einsum('qhe,khe->hqk', grad_block, value_heads, preferred_element_typ...  34.6 us
  transfers between devices with their start and end apart: 8, of which 4 were waited for; matrix products, arithmetic and copies ran while one was open for 29% of the time, Pallas kernels for 0%

commit v1 on v0

--- a/solution.py
+++ b/solution.py
@@ -4,7 +4,9 @@
 import jax
 import jax.numpy as jnp
 from jax import lax
-from jax.sharding import PartitionSpec as P
+from jax.experimental import pallas as pl
+from jax.experimental.pallas import tpu as pltpu
+from jax.sharding import Mesh, PartitionSpec as P
 
 HEADS = 16
 HEAD = 64
@@ -134,7 +136,159 @@
     return (jnp.concatenate(d_query_parts, 0), d_keys, d_values)
 
 
+AXES = ("y", "core", "z", "x")
+
+
+def ring(num):
+    return [(place, (place + 1) % num) for place in range(num)]
+
+
+class Grid:
+    def __init__(self, sizes):
+        self.sizes = dict(zip(AXES, sizes))
+        self.total = math.prod(sizes)
+
+    def coords(self):
+        return {name: lax.axis_index(name) for name in AXES}
+
+    def block(self, coords):
+        place = 0
+        for name in AXES:
+            place = place * self.sizes[name] + coords[name]
+        return place
+
+
+def gather_pieces(grid, own, order):
+    held = [own[None]]
+    for name in order:
+        held = [jnp.concatenate(held, 0) if len(held) > 1 else held[0]]
+        for _ in range(grid.sizes[name] - 1):
+            held.append(lax.ppermute(held[-1], name, ring(grid.sizes[name])))
+    return held
+
+
+def block_places(grid, coords, order, piece):
+    sizes = [grid.sizes[name] for name in order]
+    inner = math.prod(sizes[:-1])
+    places = []
+    for slot in range(inner):
+        here = dict(coords)
+        left = slot
+        for name, size in zip(order[:-1], sizes[:-1]):
+            here[name] = lax.rem(coords[name] - left % size + size, size)
+            left //= size
+        here[order[-1]] = lax.rem(coords[order[-1]] - piece + sizes[-1], sizes[-1])
+        places.append(grid.block(here))
+    return places
+
+
+def assemble_kernel(plan, num_in, *refs):
+    places, ins, outs, sem = refs[0], refs[1 : 1 + num_in], refs[1 + num_in : -1], refs[-1]
+    copies = []
+    for number, (block_id, cuts) in enumerate(plan):
+        source, slot = block_id
+        rows = ins[source].shape[1]
+        for first, width, target, column in cuts:
+            start = pl.multiple_of(places[number] * rows, rows)
+            copies.append(
+                pltpu.make_async_copy(
+                    ins[source].at[slot, :, pl.ds(first, width)],
+                    outs[target].at[pl.ds(start, rows), pl.ds(column, width)],
+                    sem,
+                )
+            )
+    for copy in copies:
+        copy.start()
+    for copy in copies:
+        copy.wait()
+
+
+def assemble(grid, coords, gathered, widths):
+    rows = gathered[0][0][0].shape[1]
+    arrays, plan, places = [], [], []
+    for pieces, order, cuts in gathered:
+        for number, piece in enumerate(pieces):
+            for slot, place in enumerate(block_places(grid, coords, order, number)):
+                plan.append(((len(arrays), slot), cuts))
+                places.append(place)
+            arrays.append(piece)
+    all_rows = rows * grid.total
+    if rows % 16:
+        results = []
+        for target, width in enumerate(widths):
+            columns = []
+            for pieces, order, cuts in gathered:
+                for first, size, aim, column in cuts:
+                    if aim == target:
+                        spots = jnp.stack(
+                            sum(
+                                [
+                                    block_places(grid, coords, order, number)
+                                    for number in range(len(pieces))
+                                ],
+                                [],
+                            )
+                        )
+                        stacked = jnp.concatenate(pieces, 0)[:, :, first : first + size]
+                        placed = jnp.zeros_like(stacked).at[spots].set(stacked)
+                        columns.append((column, placed.reshape(all_rows, size)))
+            columns.sort(key=lambda item: item[0])
+            results.append(jnp.concatenate([item[1] for item in columns], 1))
+        return results
+    return pl.pallas_call(
+        partial(assemble_kernel, plan, len(arrays)),
+        out_shape=[jax.ShapeDtypeStruct((all_rows, width), arrays[0].dtype) for width in widths],
+        in_specs=[pl.BlockSpec(memory_space=pltpu.SMEM)]
+        + [pl.BlockSpec(memory_space=pl.ANY)] * len(arrays),
+        out_specs=[pl.BlockSpec(memory_space=pl.ANY)] * len(widths),
+        scratch_shapes=[pltpu.SemaphoreType.DMA],
+        cost_estimate=pl.CostEstimate(
+            flops=0,
+            bytes_accessed=4 * all_rows * sum(widths),
+            transcendentals=0,
+        ),
+    )(jnp.stack(places).astype(jnp.int32), *arrays)
+
+
+def scatter_stages(grid, coords, terms, axes, order, wire):
+    axes = list(axes)
+    for name in order:
+        dim = axes.index(name)
+        size = grid.sizes[name]
+        arrived = None
+        for step in range(size - 1):
+            block = lax.rem(coords[name] + (2 * size - 1 - step), size)
+            sent = sum(
+                lax.dynamic_index_in_dim(term, block, dim, keepdims=False).astype(jnp.float32)
+                for term in terms
+            )
+            if arrived is not None:
+                sent = sent + arrived.astype(jnp.float32)
+            arrived = lax.ppermute(sent.astype(wire), name, ring(size))
+        terms = [
+            lax.dynamic_index_in_dim(term, coords[name], dim, keepdims=False) for term in terms
+        ] + [arrived]
+        axes.remove(name)
+    return sum(term.astype(jnp.float32) for term in terms)
+
+
+def weight_grad(grid, coords, rows_in, cots):
+    sizes = [grid.sizes[name] for name in AXES]
+    rows = rows_in.shape[0]
+    split = rows_in.reshape(rows, sizes[0], sizes[1], -1)
+
+    def part(core):
+        chosen = lax.dynamic_index_in_dim(split, core, 2, keepdims=False)
+        product = times_left(chosen.reshape(rows, -1), cots).astype(jnp.bfloat16)
+        return product.reshape(sizes[0], sizes[2], sizes[3], -1, cots.shape[1])
+
+    sent = part(1 - coords["core"])
+    arrived = lax.ppermute(sent, "core", ring(2))
+    return [part(coords["core"]), arrived]
+
+
 def local(
+    grid,
     cells,
     segment_ids,
     valid,
@@ -163,14 +317,59 @@
         allowed_rows(slide_ids, live_keys, row_start, block_rows)
         for row_start in range(0, num_rows, block_rows)
     ]
-    gain_one, shift_one, w_qkv, b_qv, w_out, b_out = (
-        lax.all_gather(norm1_gain, ("dp", "fsdp"), axis=0, tiled=True),
-        lax.all_gather(norm1_bias, ("dp", "fsdp"), axis=0, tiled=True),
-        lax.all_gather(qkv_weight, ("dp", "fsdp"), axis=0, tiled=True),
-        lax.all_gather(qv_bias, ("dp", "fsdp"), axis=0, tiled=True),
-        lax.all_gather(out_weight, ("dp", "fsdp"), axis=0, tiled=True),
-        lax.all_gather(out_bias, ("dp", "fsdp"), axis=0, tiled=True),
-    )
+    coords = grid.coords()
+    own_rows = qkv_weight.shape[0]
+    vectors = (
+        norm1_gain,
+        norm1_bias,
+        qv_bias,
+        out_bias,
+        norm2_gain,
+        norm2_bias,
+        up_bias,
+        down_bias,
+    )
+    packed = jnp.concatenate(vectors)
+    packed_size = packed.shape[0]
+    packed = jnp.pad(packed, (0, own_rows * 128 - packed_size)).reshape(own_rows, 128)
+    w_up = lax.all_gather(up_weight, AXES, axis=0, tiled=True)
+    order_a = ("x", "z", "y", "core")
+    order_b = ("y", "z", "x", "core")
+    first_half = gather_pieces(grid, qkv_weight[:, : 2 * model_width], order_a)
+    second_half = gather_pieces(
+        grid,
+        jnp.concatenate([qkv_weight[:, 2 * model_width :], out_weight, packed], 1),
+        order_b,
+    )
+    w_qkv, w_out, all_packed = assemble(
+        grid,
+        coords,
+        [
+            (first_half, order_a, [(0, 2 * model_width, 0, 0)]),
+            (
+                second_half,
+                order_b,
+                [
+                    (0, model_width, 0, 2 * model_width),
+                    (model_width, model_width, 1, 0),
+                    (2 * model_width, 128, 2, 0),
+                ],
+            ),
+        ],
+        [3 * model_width, model_width, 128],
+    )
+    down_own, _ = lax.optimization_barrier((down_weight, second_half[-1]))
+    down_pieces = gather_pieces(grid, down_own, order_a)
+    (w_down,) = assemble(
+        grid, coords, [(down_pieces, order_a, [(0, model_width, 0, 0)])], [model_width]
+    )
+    all_packed = all_packed.reshape(grid.total, -1)[:, :packed_size]
+    spread, first = [], 0
+    for vector in vectors:
+        size = vector.shape[0]
+        spread.append(all_packed[:, first : first + size].reshape(-1))
+        first += size
+    gain_one, shift_one, b_qv, b_out, gain_two, shift_two, b_up, b_down = spread
     cell_rows = cells.astype(jnp.float32)
     normed = norm_rows(
         cell_rows, gain_one.astype(jnp.float32), shift_one.astype(jnp.float32)
@@ -193,14 +392,6 @@
         + jnp.dot(mixed, w_out, preferred_element_type=jnp.float32)
         + b_out.astype(jnp.float32)
     )
-    gain_two, shift_two, w_up, b_up, w_down, b_down = (
-        lax.all_gather(norm2_gain, ("dp", "fsdp"), axis=0, tiled=True),
-        lax.all_gather(norm2_bias, ("dp", "fsdp"), axis=0, tiled=True),
-        lax.all_gather(up_weight, ("dp", "fsdp"), axis=0, tiled=True),
-        lax.all_gather(up_bias, ("dp", "fsdp"), axis=0, tiled=True),
-        lax.all_gather(down_weight, ("dp", "fsdp"), axis=0, tiled=True),
-        lax.all_gather(down_bias, ("dp", "fsdp"), axis=0, tiled=True),
-    )
     normed_two = norm_rows(
         inner, gain_two.astype(jnp.float32), shift_two.astype(jnp.float32)
     ).astype(jnp.bfloat16)
@@ -215,40 +406,22 @@
         + b_down.astype(jnp.float32)
     )
     out_cells = layer_out.astype(jnp.bfloat16)
-    gain_two_b, w_up_b, w_down_b = (
-        lax.all_gather(norm2_gain, ("dp", "fsdp"), axis=0, tiled=True),
-        lax.all_gather(up_weight, ("dp", "fsdp"), axis=0, tiled=True),
-        lax.all_gather(down_weight, ("dp", "fsdp"), axis=0, tiled=True),
-    )
     cot_rows = out_grad.astype(jnp.float32)
-    d_down = times_left(hidden_low, out_grad)
+    d_down = weight_grad(grid, coords, hidden_low, out_grad)
     d_down_bias = jnp.sum(cot_rows, axis=0)
-    d_hidden = times_right(out_grad, w_down_b)
+    d_hidden = times_right(out_grad, w_down)
     (d_up_full,) = gelu_back(d_hidden)
     d_up_low = d_up_full.astype(jnp.bfloat16)
-    d_up_weight = times_left(normed_two, d_up_low)
+    d_up_weight = weight_grad(grid, coords, normed_two, d_up_low)
     d_up_bias = jnp.sum(d_up_low.astype(jnp.float32), axis=0)
-    d_normed_two = times_right(d_up_low, w_up_b)
-    pull_two = norm_pull(inner, gain_two_b.astype(jnp.float32))
+    d_normed_two = times_right(d_up_low, w_up)
+    pull_two = norm_pull(inner, gain_two.astype(jnp.float32))
     d_inner_part, d_gain_two, d_shift_two = pull_two(d_normed_two)
     d_inner = cot_rows + d_inner_part
-    ffn_grads = (
-        lax.psum_scatter(d_gain_two, ("dp", "fsdp"), scatter_dimension=0, tiled=True),
-        lax.psum_scatter(d_shift_two, ("dp", "fsdp"), scatter_dimension=0, tiled=True),
-        lax.psum_scatter(d_up_weight, ("dp", "fsdp"), scatter_dimension=0, tiled=True),
-        lax.psum_scatter(d_up_bias, ("dp", "fsdp"), scatter_dimension=0, tiled=True),
-        lax.psum_scatter(d_down, ("dp", "fsdp"), scatter_dimension=0, tiled=True),
-        lax.psum_scatter(d_down_bias, ("dp", "fsdp"), scatter_dimension=0, tiled=True),
-    )
-    gain_one_b, w_qkv_b, w_out_b = (
-        lax.all_gather(norm1_gain, ("dp", "fsdp"), axis=0, tiled=True),
-        lax.all_gather(qkv_weight, ("dp", "fsdp"), axis=0, tiled=True),
-        lax.all_gather(out_weight, ("dp", "fsdp"), axis=0, tiled=True),
-    )
     d_inner_low = d_inner.astype(jnp.bfloat16)
-    d_out_weight = times_left(mixed, d_inner_low)
+    d_out_weight = weight_grad(grid, coords, mixed, d_inner_low)
     d_out_bias = jnp.sum(d_inner_low.astype(jnp.float32), axis=0)
-    d_mixed = times_right(d_inner_low, w_out_b).astype(jnp.bfloat16)
+    d_mixed = times_right(d_inner_low, w_out).astype(jnp.bfloat16)
     d_query_g, d_key_g, d_value_g = lax.map(
         partial(attend_backward, mask_blocks, block_rows, score_scale),
         (query_groups, key_groups, value_groups, group_heads(d_mixed, num_groups), lse_groups),
@@ -256,77 +429,105 @@
     d_query = ungroup(d_query_g)
     d_value = ungroup(d_value_g)
     d_qkv = jnp.concatenate([d_query, ungroup(d_key_g), d_value], axis=1)
-    d_qkv_weight = times_left(normed, d_qkv)
+    half_width = 3 * model_width // 2
+    d_qkv_first = weight_grad(grid, coords, normed, d_qkv[:, :half_width])
+    d_qkv_second = weight_grad(grid, coords, normed, d_qkv[:, half_width:])
     d_qv_bias = jnp.concatenate(
         [jnp.sum(d_query.astype(jnp.float32), axis=0), jnp.sum(d_value.astype(jnp.float32), axis=0)]
     )
-    d_normed = times_right(d_qkv, w_qkv_b)
-    pull_one = norm_pull(cell_rows, gain_one_b.astype(jnp.float32))
+    d_normed = times_right(d_qkv, w_qkv)
+    pull_one = norm_pull(cell_rows, gain_one.astype(jnp.float32))
     d_rows_part, d_gain_one, d_shift_one = pull_one(d_normed)
     cells_grad = (d_inner + d_rows_part).astype(jnp.bfloat16)
-    attn_grads = (
-        lax.psum_scatter(d_gain_one, ("dp", "fsdp"), scatter_dimension=0, tiled=True),
-        lax.psum_scatter(d_shift_one, ("dp", "fsdp"), scatter_dimension=0, tiled=True),
-        lax.psum_scatter(d_qkv_weight, ("dp", "fsdp"), scatter_dimension=0, tiled=True),
-        lax.psum_scatter(d_qv_bias, ("dp", "fsdp"), scatter_dimension=0, tiled=True),
-        lax.psum_scatter(d_out_weight, ("dp", "fsdp"), scatter_dimension=0, tiled=True),
-        lax.psum_scatter(d_out_bias, ("dp", "fsdp"), scatter_dimension=0, tiled=True),
-    )
+    left_axes = ("y", "z", "x")
+
+    def total(terms, order):
+        return scatter_stages(grid, coords, terms, left_axes, order, jnp.bfloat16)
+
+    down_total = total(d_down, ("x", "z", "y"))
+    up_total = total(d_up_weight, ("y", "z", "x"))
+    out_total = total(d_out_weight, ("x", "z", "y"))
+    qkv_total = jnp.concatenate(
+        [total(d_qkv_first, ("x", "z", "y")), total(d_qkv_second, ("y", "z", "x"))], 1
+    )
+    vector_grads = (
+        d_gain_one,
+        d_shift_one,
+        d_qv_bias,
+        d_out_bias,
+        d_gain_two,
+        d_shift_two,
+        d_up_bias,
+        d_down_bias,
+    )
+    sizes = [grid.sizes[name] for name in AXES]
+    stacked = jnp.concatenate([grad.reshape(*sizes, -1) for grad in vector_grads], -1)
+    summed = scatter_stages(
+        grid, coords, [stacked], AXES, ("core", "x", "z", "y"), jnp.float32
+    )
+    parts, first = [], 0
+    for vector in vectors:
+        parts.append(summed[first : first + vector.shape[0]])
+        first += vector.shape[0]
     return (
         out_cells,
         cells_grad,
-        attn_grads[0],
-        attn_grads[1],
-        attn_grads[2],
-        attn_grads[3],
-        attn_grads[4],
-        attn_grads[5],
-        ffn_grads[0],
-        ffn_grads[1],
-        ffn_grads[2],
-        ffn_grads[3],
-        ffn_grads[4],
-        ffn_grads[5],
+        parts[0],
+        parts[1],
+        qkv_total,
+        parts[2],
+        out_total,
+        parts[3],
+        parts[4],
+        parts[5],
+        up_total,
+        parts[6],
+        down_total,
+        parts[7],
     )
 
 
 def solution(mesh):
+    outer, inner_size = mesh.devices.shape
+    sizes = (outer // 2, 2, inner_size // 2, 2)
+    fine = Mesh(mesh.devices.reshape(sizes), AXES)
+    rows, vector = P(AXES, None), P(AXES)
     return jax.shard_map(
-        local,
-        mesh=mesh,
+        partial(local, Grid(sizes)),
+        mesh=fine,
         in_specs=(
-            P(("dp", "fsdp"), None),
-            P(("dp", "fsdp"), None),
-            P(("dp", "fsdp"), None),
-            P(("dp", "fsdp")),
-            P(("dp", "fsdp")),
-            P(("dp", "fsdp"), None),
-            P(("dp", "fsdp")),
-            P(("dp", "fsdp"), None),
-            P(("dp", "fsdp")),
-            P(("dp", "fsdp")),
-            P(("dp", "fsdp")),
-            P(("dp", "fsdp"), None),
-            P(("dp", "fsdp")),
-            P(("dp", "fsdp"), None),
-            P(("dp", "fsdp")),
-            P(("dp", "fsdp"), None),
+            rows,
+            rows,
+            rows,
+            vector,
+            vector,
+            rows,
+            vector,
+            rows,
+            vector,
+            vector,
+            vector,
+            rows,
+            vector,
+            rows,
+            vector,
+            rows,
         ),
         out_specs=(
-            P(("dp", "fsdp"), None),
-            P(("dp", "fsdp"), None),
-            P(("dp", "fsdp")),
-            P(("dp", "fsdp")),
-            P(("dp", "fsdp"), None),
-            P(("dp", "fsdp")),
-            P(("dp", "fsdp"), None),
-            P(("dp", "fsdp")),
-            P(("dp", "fsdp")),
-            P(("dp", "fsdp")),
-            P(("dp", "fsdp"), None),
-            P(("dp", "fsdp")),
-            P(("dp", "fsdp"), None),
-            P(("dp", "fsdp")),
+            rows,
+            rows,
+            vector,
+            vector,
+            rows,
+            vector,
+            rows,
+            vector,
+            vector,
+            vector,
+            rows,
+            vector,
+            rows,
+            vector,
         ),
         check_vma=False,
     )

time: 1450 us -> 1440 us (level)
  waiting for transfers between devices: 764 us -> 229 us
  Pallas kernels: 0 us -> 520 us
  blocking collectives: 149 us -> 0 us
  local copies, waits for them, and re-layouts: 97.7 us -> 191 us
  starting transfers between devices: 0.31 us -> 33.7 us
  other arithmetic: 113 us -> 134 us
    reduce_scatter x4 -> x0, waiting for transfers between devices: 728 us -> none  [the longest x1 360 us: local(): lax.psum_scatter(d_down, ('dp', 'fsdp'), scatter_dimension=0, tiled=True)]
    pallas_call x0 -> x2, Pallas kernels: none -> 520 us  [assemble(): pl.pallas_call(partial(assemble_kernel, plan, len(arrays)), out_shape=[ja...]
    ppermute x0 -> x54, waiting for transfers between devices: none -> 229 us  [the longest x31 120 us: scatter_stages(): arrived = lax.ppermute(sent.astype(wire), name, ring(size))]
    unnamed x2 -> x0, blocking collectives: 83.6 us -> none
    all_gather x1 -> x0, blocking collectives: 65.6 us -> none  [local(): lax.all_gather(up_bias, ('dp', 'fsdp'), axis=0, tiled=True)]
    ppermute x0 -> x54, starting transfers between devices: none -> 33.6 us  [the longest x31 21.1 us: scatter_stages(): arrived = lax.ppermute(sent.astype(wire), name, ring(size))]
    all_gather x4 -> x1, waiting for transfers between devices: 33.1 us -> 0.02 us  [local(): w_up = lax.all_gather(up_weight, AXES, axis=0, tiled=True)]
    unnamed x152 -> x167, local copies, waits for them, and re-layouts: 35 us -> 67.9 us
  transfers between devices with their start and end apart: 8 -> 55, of which waited for: 4 -> 32; matrix products, arithmetic and copies ran while one was open for 29% -> 21% of each run, Pallas kernels for 0% -> 36%
where the time goes in v1:
time: 1440 us; the launch traced here: 1430 us
  Pallas kernels  520 us (36%)
  matrix products  306 us (21%)
  waiting for transfers between devices  229 us (16%)
  local copies, waits for them, and re-layouts  191 us (13%)
  other arithmetic  134 us (9%)
  starting transfers between devices  33.7 us (2%)
  between operations  15.6 us (1%)
    pallas_call x2, Pallas kernels, assemble(): pl.pallas_call(partial(assemble_kernel, plan, len(arrays)), out_shape=[ja...  520 us
    ppermute x31, waiting for transfers between devices, scatter_stages(): arrived = lax.ppermute(sent.astype(wire), name, ring(size))  120 us
    ppermute x18, waiting for transfers between devices, gather_pieces(): held.append(lax.ppermute(held[-1], name, ring(grid.sizes[name])))  108 us
    unnamed x167, local copies, waits for them, and re-layouts  67.9 us
    dot_general x4, matrix products, times_right(): lax.dot_general(left_mat, right_mat, (((1,), (1,)), ((), ())), preferred_...  54.9 us
    dot_general x10, matrix products, times_left(): lax.dot_general(left_mat, right_mat, (((0,), (0,)), ((), ())), preferred_...  54.6 us
    dot_general x1, matrix products, local(): jnp.dot(normed_two, w_up, preferred_element_type=jnp.float32)  48 us
    dot_general x8, matrix products, attend_backward(): jnp.einsum('qhe,khe->hqk', grad_block, value_heads, preferred_element_typ...  34.8 us
  transfers between devices with their start and end apart: 55, of which 32 were waited for; matrix products, arithmetic and copies ran while one was open for 21% of the time, Pallas kernels for 36%

profile of v1, /device:TPU:0, one launch (start us, length us, event | category | flops | bytes accessed | tf_op | source)
XLA Modules:
  0.0 1430.6 jit_solution(14845129112197854927)
XLA Ops:
  39.3 9.1 collective-permute-done.8
  49.2 8.0 collective-permute-done.9
  69.5 12.4 collective-permute-done.10
  83.0 6.8 collective-permute-done.4
  110.2 263.9 %shard_map.263 = (bf16[1024,3072]{1,0:T(8,128)(2,1)}, bf16[1024,1024]{1,0:T(8,128)(2,1)}, bf16[1024,128]{1,0:T(8,128)(2,1)}) custom-call(s32[64]{0:T(128)} %stack.198.refs_0_, bf16[16,32,2048]{2,1,0:T(8,128)(2,1)} %constant_dynamic-update-slice_fusion.7.refs_1_, bf16[16,32,2048]{2,1,0:T(8,128)(2,1)} %collective-permute-done.5.refs_2_, ...), custom_call_target="tpu_custom_call" | custom-call | bytes 17301504 | tf_op jit(solution)/shard_map/pallas_call | solution.py:238
  379.1 12.4 collective-permute-done.14
  394.9 11.4 collective-permute-done.15
  408.4 8.9 fusion.160
  431.4 21.9 %collective-permute-done.16 = bf16[8,128,1024]{2,1,0:T(8,128)(2,1)} collective-permute-done((bf16[8,128,1024]{2,1,0:T(8,128)(2,1)}, bf16[8,128,1024]{2,1,0:T(8,128)(2,1)}, u32[]{:S(2)}, u32[]{:S(2)}) %collective-permute-start.16) | collective-permute-done | bytes 2097184 | tf_op jit(solution)/shard_map/ppermute | solution.py:166
  458.0 77.3 %while.30 = (s32[]{:T(128)}, bf16[4,1024,256]{1,2,0:T(8,128)(2,1)}, f32[4,4,1024]{2,1,0:T(4,128)}, bf16[4,1024,256]{1,2,0:T(8,128)(2,1)}, bf16[4,1024,256]{1,2,0...) while((s32[]{:T(128)}, bf16[4,1024,256]{1,2,0:T(8,128)(2,1)}, ...), condition=%wide.region_7.8_spmd.clone.clone, body=%wide.region_2.7_spmd.clone.clone.sunk | while | flops 1129578496 | bytes 62041260 | solution.py:385
  550.3 255.9 %shard_map.264 = bf16[4096,1024]{1,0:T(8,128)(2,1)} custom-call(s32[32]{0:T(128)} %stack.199.refs_0_, bf16[16,128,1024]{2,1,0:T(8,128)(2,1)} %constant_dynamic-update-slice_fusion.29.refs_1_, bf16[16,128,1024]{2,1,0:T(8,128)(2,1)} %collective-permute-done.17.refs_2_), custom_call_target="tpu_custom_call" | custom-call | bytes 16777216 | tf_op jit(solution)/shard_map/pallas_call | solution.py:238
  806.3 48.0 %multiply_convert_fusion.2 = (bf16[1024,4096]{1,0:T(8,128)(2,1)}, f32[1024,4096]{1,0:T(8,128)}, f32[1024,4096]{1,0:T(8,128)}) fusion(f32[4096]{0:T(1024)S(1)} %fusion.129, bf16[1024,1024]{0,1:T(8,128)(2,1)S(1)} %add_convert_fusion.4, bf16[1024,4096]{1,0:T(8,128)(2,1)} %all-gather.2.cloned.1.call-done), kind=kOutput, calls=%fused_computation.92 | convolution fusion | flops 8866758656 | bytes 52445184 | tf_op jit(solution)/shard_map/dot_general | solution.py:398
  854.3 24.3 %convert_reduce_fusion = (f32[4096]{0:T(1024)}, bf16[1024,4096]{1,0:T(8,128)(2,1)}) fusion(f32[1024,4096]{1,0:T(8,128)} %get-tuple-element.366, bf16[4096,1024]{1,0:T(8,128)(2,1)} %shard_map.264, bf16[1024,1024]{1,0:T(8,128)(2,1)S(1)} %copy-done.21, f32[1024,4096]{1,0:T(8,128)} %get-tuple-element.460, f32[4096]{0:T(1024)S(1)} %fusion.129), kind=kOutput, calls=%fused_computation.91 | convolution fusion | flops 8661233664 | bytes 52461568 | tf_op jit(solution)/shard_map/dot_general | solution.py:42
  878.6 15.7 %fusion.156 = (f32[1024]{0:T(1024)}, f32[1024,1024]{1,0:T(8,128)}) fusion(bf16[1024,4096]{1,0:T(8,128)(2,1)} %get-tuple-element.466, bf16[1024,4096]{1,0:T(8,128)(2,1)} %all-gather.2.cloned.1.call-done), kind=kOutput, calls=%fused_computation.362 | convolution fusion | flops 8590982144 | bytes 20975616 | tf_op jit(solution)/shard_map/dot_general | solution.py:42
  916.9 144.2 %while.31 = (s32[]{:T(128)}, bf16[4,1024,256]{1,2,0:T(8,128)(2,1)}, bf16[4,1024,256]{1,2,0:T(8,128)(2,1)}, bf16[4,1024,256]{1,2,0:T(8,128)(2,1)S(1)}, bf16[4,102...) while((s32[]{:T(128)}, bf16[4,1024,256]{1,2,0:T(8,128)(2,1)}, ...), condition=%wide.region_15.16_spmd.clone.clone, body=%wide.region_12.15_spmd.clone.clone.sunk | while | flops 2754342912 | bytes 148532432 | solution.py:425
  1064.0 11.2 fusion.155
  1081.2 14.4 %reshape.730 = bf16[1024,2,2,1024]{3,2,1,0:T(2,128)(2,1)} reshape(bf16[1024,4096]{1,0:T(8,128)(2,1)} %get-tuple-element.365) | data formatting | bytes 16777216 | tf_op jit(solution)/shard_map/reshape | solution.py:278
  1095.6 15.6 %add_convert_fusion.3 = bf16[1024,1024]{0,1:T(8,128)(2,1)} fusion(f32[1024,1024]{0,1:T(8,128)} %copy-done.4, f32[1024]{0:T(1024)S(1)} %copy-done.70, bf16[1024,4096]{1,0:T(8,128)(2,1)} %get-tuple-element.365, bf16[4096,1024]{1,0:T(8,128)(2,1)} %shard_map.264), kind=kOutput, calls=%fused_computation.146 | convolution fusion | flops 8593080320 | bytes 23072768 | tf_op jit(solution)/shard_map/dot_general | solution.py:405
  1111.4 9.6 convolution_convert_fusion.1
  1121.0 9.4 convolution_convert_fusion
  1156.4 20.3 %constant_dynamic-slice_fusion.11 = (bf16[1024,2,1,1024]{3,2,1,0:T(2,128)(2,1)}, bf16[1024,2,1,1024]{3,2,1,0:T(2,128)(2,1)}) fusion(bf16[1024,2,2,1024]{3,2,1,0:T(2,128)(2,1)} %reshape.730, s32[]{:T(128)S(6)} %select_n.231, s32[]{:T(128)S(6)} %select_n.248), kind=kLoop, calls=%fused_computation.280 | loop fusion | bytes 16777224 | tf_op jit(solution)/shard_map/jit(dynamic_index_in_dim)/dynamic_slice | solution.py:281
  1176.7 20.1 %copy.127 = bf16[1024,2,1,1024]{0,3,1,2:T(8,128)(2,1)} copy(bf16[1024,2,1,1024]{3,2,1,0:T(2,128)(2,1)} %get-tuple-element.393) | data formatting | bytes 8388608
  1196.8 8.3 convolution_convert_fusion.3
  1205.2 20.0 %copy.128 = bf16[1024,2,1,1024]{0,3,1,2:T(8,128)(2,1)} copy(bf16[1024,2,1,1024]{3,2,1,0:T(2,128)(2,1)} %get-tuple-element.394) | data formatting | bytes 8388608
  1229.0 8.5 convolution_convert_fusion.2
  1295.7 11.6 collective-permute-done.31
  1324.0 22.8 %collective-permute-done.43 = bf16[4,2,32,4096]{3,2,1,0:T(8,128)(2,1)S(1)} collective-permute-done((bf16[4,2,32,4096]{3,2,1,0:T(8,128)(2,1)S(1)}, bf16[4,2,32,4096]{3,2,1,0:T(8,128)(2,1)S(1)}, u32[]{:S(2)}, u32[]{:S(2)}) %collective-permute-start.43) | collective-permute-done | bytes 2097184 | tf_op jit(solution)/shard_map/ppermute | solution.py:267
  1353.6 11.2 collective-permute-done.44
  1367.1 8.9 collective-permute-done.50
  1377.5 9.8 collective-permute-done.45
  1388.7 9.8 collective-permute-done.51
  1400.0 8.5 collective-permute-done.46
  (533 shorter events, 494.5 us)
Async XLA Ops:
  7.2 799.1 %all-gather.2.cloned.1.call-start = ((), (), s32[]{:S(2)}) async-start(), calls=%async_computation | async-start | bytes 8650752 | tf_op jit(solution)/shard_map/all_gather | solution.py:335
  23.6 15.0 %collective-permute-start.7 = (bf16[2,32,2176]{2,1,0:T(8,128)(2,1)S(1)}, bf16[2,32,2176]{2,1,0:T(8,128)(2,1)S(1)}, u32[]{:S(2)}, u32[]{:S(2)}) collective-permute-start(bf16[2,32,2176]{2,1,0:T(8,128)(2,1)S(1)} %pad_maximum_fusion.8), channel_id=1, source_target_pairs={{0,2},{2,4},{4,6},{6,0},{1,3},{3,5},{5,7},{7,1},{8,10},{10,12},{12... | collective-permute-start | bytes 835592 | tf_op jit(solution)/shard_map/ppermute | solution.py:166
  32.6 27.3 %collective-permute-start.2 = (bf16[2,32,2048]{2,1,0:T(8,128)(2,1)S(1)}, bf16[2,32,2048]{2,1,0:T(8,128)(2,1)S(1)}, u32[]{:S(2)}, u32[]{:S(2)}) collective-permute-start(bf16[2,32,2048]{2,1,0:T(8,128)(2,1)S(1)} %collective-permute-done.1), channel_id=1, source_target_pairs={{0,2},{2,4},{4,6},{6,0},{1,3},{3,5},{5,7},{7,1},{8,10},{10,12},{12... | collective-permute-start | bytes 786440 | tf_op jit(solution)/shard_map/ppermute | solution.py:166
  57.9 24.0 %collective-permute-start.10 = (bf16[8,32,2176]{2,1,0:T(8,128)(2,1)S(1)}, bf16[8,32,2176]{2,1,0:T(8,128)(2,1)S(1)}, u32[]{:S(2)}, u32[]{:S(2)}) collective-permute-start(bf16[8,32,2176]{2,1,0:T(8,128)(2,1)S(1)} %get-tuple-element.409), channel_id=1, source_target_pairs={{0,1},{1,0},{2,3},{3,2},{4,5},{5,4},{6,7},{7,6},{8,9},{9,8},{10,11... | collective-permute-start | bytes 3342344 | tf_op jit(solution)/shard_map/ppermute | solution.py:166
  68.7 21.1 %collective-permute-start.4 = (bf16[8,32,2048]{2,1,0:T(8,128)(2,1)S(1)}, bf16[8,32,2048]{2,1,0:T(8,128)(2,1)S(1)}, u32[]{:S(2)}, u32[]{:S(2)}) collective-permute-start(bf16[8,32,2048]{2,1,0:T(8,128)(2,1)S(1)} %get-tuple-element.425), channel_id=1, source_target_pairs={{0,16},{16,0},{1,17},{17,1},{2,18},{18,2},{3,19},{19,3},{4,20},{20... | collective-permute-start | bytes 3145736 | tf_op jit(solution)/shard_map/ppermute | solution.py:166
  83.0 17.5 %collective-permute-start.11 = (bf16[16,32,2176]{2,1,0:T(8,128)(2,1)}, bf16[16,32,2176]{2,1,0:T(8,128)(2,1)}, u32[]{:S(2)}, u32[]{:S(2)}) collective-permute-start(bf16[16,32,2176]{2,1,0:T(8,128)(2,1)} %constant_dynamic-update-slice_fusion.18.refs_3_), channel_id=1, source_target_pairs={{0,8},{8,0},{1,9},{9,1},{2,10},{10,2},{3,11},{11,3},{4,12},{12,4},... | collective-permute-start | bytes 6684680 | tf_op jit(solution)/shard_map/ppermute | solution.py:166
  91.0 19.2 %collective-permute-start.5 = (bf16[16,32,2048]{2,1,0:T(8,128)(2,1)}, bf16[16,32,2048]{2,1,0:T(8,128)(2,1)}, u32[]{:S(2)}, u32[]{:S(2)}) collective-permute-start(bf16[16,32,2048]{2,1,0:T(8,128)(2,1)} %constant_dynamic-update-slice_fusion.7.refs_1_), channel_id=1, source_target_pairs={{0,8},{8,0},{1,9},{9,1},{2,10},{10,2},{3,11},{11,3},{4,12},{12,4},... | collective-permute-start | bytes 6291464 | tf_op jit(solution)/shard_map/ppermute | solution.py:166
  110.2 265.9 %collective-permute-start.13 = (bf16[2,128,1024]{2,1,0:T(8,128)(2,1)}, bf16[2,128,1024]{2,1,0:T(8,128)(2,1)S(1)}, u32[]{:S(2)}, u32[]{:S(2)}) collective-permute-start(bf16[2,128,1024]{2,1,0:T(8,128)(2,1)} %pad_maximum_fusion.6), channel_id=1, source_target_pairs={{0,2},{2,4},{4,6},{6,0},{1,3},{3,5},{5,7},{7,1},{8,10},{10,12},{12... | collective-permute-start | bytes 1572872 | tf_op jit(solution)/shard_map/ppermute | solution.py:166
  376.0 15.5 %collective-permute-start.14 = (bf16[2,128,1024]{2,1,0:T(8,128)(2,1)S(1)}, bf16[2,128,1024]{2,1,0:T(8,128)(2,1)S(1)}, u32[]{:S(2)}, u32[]{:S(2)}) collective-permute-start(bf16[2,128,1024]{2,1,0:T(8,128)(2,1)S(1)} %collective-permute-done.13), channel_id=1, source_target_pairs={{0,2},{2,4},{4,6},{6,0},{1,3},{3,5},{5,7},{7,1},{8,10},{10,12},{12... | collective-permute-start | bytes 1572872 | tf_op jit(solution)/shard_map/ppermute | solution.py:166
  391.5 14.8 %collective-permute-start.15 = (bf16[2,128,1024]{2,1,0:T(8,128)(2,1)S(1)}, bf16[2,128,1024]{2,1,0:T(8,128)(2,1)S(1)}, u32[]{:S(2)}, u32[]{:S(2)}) collective-permute-start(bf16[2,128,1024]{2,1,0:T(8,128)(2,1)S(1)} %collective-permute-done.14), channel_id=1, source_target_pairs={{0,2},{2,4},{4,6},{6,0},{1,3},{3,5},{5,7},{7,1},{8,10},{10,12},{12... | collective-permute-start | bytes 1572872 | tf_op jit(solution)/shard_map/ppermute | solution.py:166
  407.4 45.9 %collective-permute-start.16 = (bf16[8,128,1024]{2,1,0:T(8,128)(2,1)}, bf16[8,128,1024]{2,1,0:T(8,128)(2,1)}, u32[]{:S(2)}, u32[]{:S(2)}) collective-permute-start(bf16[8,128,1024]{2,1,0:T(8,128)(2,1)} %get-tuple-element.403), channel_id=1, source_target_pairs={{0,16},{16,0},{1,17},{17,1},{2,18},{18,2},{3,19},{19,3},{4,20},{20... | collective-permute-start | bytes 6291464 | tf_op jit(solution)/shard_map/ppermute | solution.py:166
  456.4 94.0 %collective-permute-start.17 = (bf16[16,128,1024]{2,1,0:T(8,128)(2,1)}, bf16[16,128,1024]{2,1,0:T(8,128)(2,1)}, u32[]{:S(2)}, u32[]{:S(2)}) collective-permute-start(bf16[16,128,1024]{2,1,0:T(8,128)(2,1)} %constant_dynamic-update-slice_fusion.29.refs_1_), channel_id=1, source_target_pairs={{0,8},{8,0},{1,9},{9,1},{2,10},{10,2},{3,11},{11,3},{4,12},{12,4},... | collective-permute-start | bytes 12582920 | tf_op jit(solution)/shard_map/ppermute | solution.py:166
  1135.1 108.1 %collective-permute-start.36 = (bf16[2,4,2,32,1024]{4,3,2,1,0:T(8,128)(2,1)}, bf16[2,4,2,32,1024]{4,3,2,1,0:T(8,128)(2,1)}, u32[]{:S(2)}, u32[]{:S(2)}) collective-permute-start(bf16[2,4,2,32,1024]{4,3,2,1,0:T(8,128)(2,1)} %bitcast.640), channel_id=1, source_target_pairs={{0,8},{8,0},{1,9},{9,1},{2,10},{10,2},{3,11},{11,3},{4,12},{12,4},... | collective-permute-start | bytes 3145736 | tf_op jit(solution)/shard_map/ppermute | solution.py:286
  1139.9 130.3 %collective-permute-start.24 = (bf16[2,4,2,32,1536]{4,3,2,1,0:T(8,128)(2,1)}, bf16[2,4,2,32,1536]{4,3,2,1,0:T(8,128)(2,1)}, u32[]{:S(2)}, u32[]{:S(2)}) collective-permute-start(bf16[2,4,2,32,1536]{4,3,2,1,0:T(8,128)(2,1)} %bitcast.68), channel_id=1, source_target_pairs={{0,8},{8,0},{1,9},{9,1},{2,10},{10,2},{3,11},{11,3},{4,12},{12,4},... | collective-permute-start | bytes 4718600 | tf_op jit(solution)/shard_map/ppermute | solution.py:286
  1155.7 69.4 %collective-permute-start.18 = (f32[2,4,2,384]{3,2,1,0:T(2,128)S(1)}, f32[2,4,2,384]{3,2,1,0:T(2,128)S(1)}, u32[]{:S(2)}, u32[]{:S(2)}) collective-permute-start(f32[2,4,2,384]{3,2,1,0:T(2,128)S(1)} %fusion.128), channel_id=1, source_target_pairs={{0,8},{8,0},{1,9},{9,1},{2,10},{10,2},{3,11},{11,3},{4,12},{12,4},... | collective-permute-start | bytes 73736 | tf_op jit(solution)/shard_map/ppermute | solution.py:267
  1156.3 136.0 %collective-permute-start.42 = (bf16[2,4,2,32,4096]{4,3,2,1,0:T(8,128)(2,1)}, bf16[2,4,2,32,4096]{4,3,2,1,0:T(8,128)(2,1)}, u32[]{:S(2)}, u32[]{:S(2)}) collective-permute-start(bf16[2,4,2,32,4096]{4,3,2,1,0:T(8,128)(2,1)} %bitcast.638), channel_id=1, source_target_pairs={{0,8},{8,0},{1,9},{9,1},{2,10},{10,2},{3,11},{11,3},{4,12},{12,4},... | collective-permute-start | bytes 12582920 | tf_op jit(solution)/shard_map/ppermute | solution.py:286
  1239.0 69.5 %collective-permute-start.48 = (bf16[2,4,2,128,1024]{4,3,2,1,0:T(8,128)(2,1)}, bf16[2,4,2,128,1024]{4,3,2,1,0:T(8,128)(2,1)}, u32[]{:S(2)}, u32[]{:S(2)}) collective-permute-start(bf16[2,4,2,128,1024]{4,3,2,1,0:T(8,128)(2,1)} %bitcast.138), channel_id=1, source_target_pairs={{0,8},{8,0},{1,9},{9,1},{2,10},{10,2},{3,11},{11,3},{4,12},{12,4},... | collective-permute-start | bytes 12582920 | tf_op jit(solution)/shard_map/ppermute | solution.py:286
  1256.5 28.8 %collective-permute-start.30 = (bf16[2,4,2,32,1536]{4,3,2,1,0:T(8,128)(2,1)}, bf16[2,4,2,32,1536]{4,3,2,1,0:T(8,128)(2,1)S(1)}, u32[]{:S(2)}, u32[]{:S(2)}) collective-permute-start(bf16[2,4,2,32,1536]{4,3,2,1,0:T(8,128)(2,1)} %bitcast.639), channel_id=1, source_target_pairs={{0,8},{8,0},{1,9},{9,1},{2,10},{10,2},{3,11},{11,3},{4,12},{12,4},... | collective-permute-start | bytes 4718600 | tf_op jit(solution)/shard_map/ppermute | solution.py:286
  1271.8 19.4 %collective-permute-start.25 = (bf16[2,4,32,1536]{3,2,1,0:T(8,128)(2,1)S(1)}, bf16[2,4,32,1536]{3,2,1,0:T(8,128)(2,1)S(1)}, u32[]{:S(2)}, u32[]{:S(2)}) collective-permute-start(bf16[2,4,32,1536]{3,2,1,0:T(8,128)(2,1)S(1)} %fusion.99), channel_id=1, source_target_pairs={{0,1},{1,0},{2,3},{3,2},{4,5},{5,4},{6,7},{7,6},{8,9},{9,8},{10,11... | collective-permute-start | bytes 2359304 | tf_op jit(solution)/shard_map/ppermute | solution.py:267
  1286.7 20.5 %collective-permute-start.31 = (bf16[4,2,32,1536]{3,2,1,0:T(8,128)(2,1)S(1)}, bf16[4,2,32,1536]{3,2,1,0:T(8,128)(2,1)S(1)}, u32[]{:S(2)}, u32[]{:S(2)}) collective-permute-start(bf16[4,2,32,1536]{3,2,1,0:T(8,128)(2,1)S(1)} %fusion.100), channel_id=1, source_target_pairs={{0,16},{16,0},{1,17},{17,1},{2,18},{18,2},{3,19},{19,3},{4,20},{20... | collective-permute-start | bytes 2359304 | tf_op jit(solution)/shard_map/ppermute | solution.py:267
  1292.2 15.2 %collective-permute-start.26 = (bf16[2,32,1536]{2,1,0:T(8,128)(2,1)S(1)}, bf16[2,32,1536]{2,1,0:T(8,128)(2,1)S(1)}, u32[]{:S(2)}, u32[]{:S(2)}) collective-permute-start(bf16[2,32,1536]{2,1,0:T(8,128)(2,1)S(1)} %fusion.112), channel_id=1, source_target_pairs={{0,2},{2,4},{4,6},{6,0},{1,3},{3,5},{5,7},{7,1},{8,10},{10,12},{12... | collective-permute-start | bytes 589832 | tf_op jit(solution)/shard_map/ppermute | solution.py:267
  1294.9 52.0 %collective-permute-start.43 = (bf16[4,2,32,4096]{3,2,1,0:T(8,128)(2,1)S(1)}, bf16[4,2,32,4096]{3,2,1,0:T(8,128)(2,1)S(1)}, u32[]{:S(2)}, u32[]{:S(2)}) collective-permute-start(bf16[4,2,32,4096]{3,2,1,0:T(8,128)(2,1)S(1)} %fusion.87), channel_id=1, source_target_pairs={{0,16},{16,0},{1,17},{17,1},{2,18},{18,2},{3,19},{19,3},{4,20},{20... | collective-permute-start | bytes 6291464 | tf_op jit(solution)/shard_map/ppermute | solution.py:267
  1311.1 41.1 %collective-permute-start.49 = (bf16[2,4,128,1024]{3,2,1,0:T(8,128)(2,1)S(1)}, bf16[2,4,128,1024]{3,2,1,0:T(8,128)(2,1)S(1)}, u32[]{:S(2)}, u32[]{:S(2)}) collective-permute-start(bf16[2,4,128,1024]{3,2,1,0:T(8,128)(2,1)S(1)} %fusion.88), channel_id=1, source_target_pairs={{0,1},{1,0},{2,3},{3,2},{4,5},{5,4},{6,7},{7,6},{8,9},{9,8},{10,11... | collective-permute-start | bytes 6291464 | tf_op jit(solution)/shard_map/ppermute | solution.py:267
  1320.1 28.1 %collective-permute-start.28 = (bf16[2,32,1536]{2,1,0:T(8,128)(2,1)S(1)}, bf16[2,32,1536]{2,1,0:T(8,128)(2,1)S(1)}, u32[]{:S(2)}, u32[]{:S(2)}) collective-permute-start(bf16[2,32,1536]{2,1,0:T(8,128)(2,1)S(1)} %fusion.116), channel_id=1, source_target_pairs={{0,2},{2,4},{4,6},{6,0},{1,3},{3,5},{5,7},{7,1},{8,10},{10,12},{12... | collective-permute-start | bytes 589832 | tf_op jit(solution)/shard_map/ppermute | solution.py:267
  1324.0 26.7 %collective-permute-start.34 = (bf16[2,32,1536]{2,1,0:T(8,128)(2,1)S(1)}, bf16[2,32,1536]{2,1,0:T(8,128)(2,1)S(1)}, u32[]{:S(2)}, u32[]{:S(2)}) collective-permute-start(bf16[2,32,1536]{2,1,0:T(8,128)(2,1)S(1)} %fusion.111), channel_id=1, source_target_pairs={{0,2},{2,4},{4,6},{6,0},{1,3},{3,5},{5,7},{7,1},{8,10},{10,12},{12... | collective-permute-start | bytes 589832 | tf_op jit(solution)/shard_map/ppermute | solution.py:267
  1348.1 16.7 %collective-permute-start.44 = (bf16[2,32,4096]{2,1,0:T(8,128)(2,1)S(1)}, bf16[2,32,4096]{2,1,0:T(8,128)(2,1)S(1)}, u32[]{:S(2)}, u32[]{:S(2)}) collective-permute-start(bf16[2,32,4096]{2,1,0:T(8,128)(2,1)S(1)} %fusion.94), channel_id=1, source_target_pairs={{0,2},{2,4},{4,6},{6,0},{1,3},{3,5},{5,7},{7,1},{8,10},{10,12},{12... | collective-permute-start | bytes 1572872 | tf_op jit(solution)/shard_map/ppermute | solution.py:267
  1349.1 17.0 %collective-permute-start.29 = (bf16[32,1536]{1,0:T(8,128)(2,1)S(1)}, bf16[32,1536]{1,0:T(8,128)(2,1)S(1)}, u32[]{:S(2)}, u32[]{:S(2)}) collective-permute-start(bf16[32,1536]{1,0:T(8,128)(2,1)S(1)} %fusion.124), channel_id=1, source_target_pairs={{0,16},{16,0},{1,17},{17,1},{2,18},{18,2},{3,19},{19,3},{4,20},{20... | collective-permute-start | bytes 294920 | tf_op jit(solution)/shard_map/ppermute | solution.py:267
  1350.8 37.9 %collective-permute-start.35 = (bf16[32,1536]{1,0:T(8,128)(2,1)S(1)}, bf16[32,1536]{1,0:T(8,128)(2,1)S(1)}, u32[]{:S(2)}, u32[]{:S(2)}) collective-permute-start(bf16[32,1536]{1,0:T(8,128)(2,1)S(1)} %fusion.122), channel_id=1, source_target_pairs={{0,1},{1,0},{2,3},{3,2},{4,5},{5,4},{6,7},{7,6},{8,9},{9,8},{10,11... | collective-permute-start | bytes 294920 | tf_op jit(solution)/shard_map/ppermute | solution.py:267
  1353.5 22.5 %collective-permute-start.50 = (bf16[2,128,1024]{2,1,0:T(8,128)(2,1)S(1)}, bf16[2,128,1024]{2,1,0:T(8,128)(2,1)S(1)}, u32[]{:S(2)}, u32[]{:S(2)}) collective-permute-start(bf16[2,128,1024]{2,1,0:T(8,128)(2,1)S(1)} %fusion.89), channel_id=1, source_target_pairs={{0,2},{2,4},{4,6},{6,0},{1,3},{3,5},{5,7},{7,1},{8,10},{10,12},{12... | collective-permute-start | bytes 1572872 | tf_op jit(solution)/shard_map/ppermute | solution.py:267
  1366.1 21.2 %collective-permute-start.45 = (bf16[2,32,4096]{2,1,0:T(8,128)(2,1)S(1)}, bf16[2,32,4096]{2,1,0:T(8,128)(2,1)S(1)}, u32[]{:S(2)}, u32[]{:S(2)}) collective-permute-start(bf16[2,32,4096]{2,1,0:T(8,128)(2,1)S(1)} %fusion.96), channel_id=1, source_target_pairs={{0,2},{2,4},{4,6},{6,0},{1,3},{3,5},{5,7},{7,1},{8,10},{10,12},{12... | collective-permute-start | bytes 1572872 | tf_op jit(solution)/shard_map/ppermute | solution.py:267
  1377.4 21.1 %collective-permute-start.51 = (bf16[2,128,1024]{2,1,0:T(8,128)(2,1)S(1)}, bf16[2,128,1024]{2,1,0:T(8,128)(2,1)S(1)}, u32[]{:S(2)}, u32[]{:S(2)}) collective-permute-start(bf16[2,128,1024]{2,1,0:T(8,128)(2,1)S(1)} %fusion.91), channel_id=1, source_target_pairs={{0,2},{2,4},{4,6},{6,0},{1,3},{3,5},{5,7},{7,1},{8,10},{10,12},{12... | collective-permute-start | bytes 1572872 | tf_op jit(solution)/shard_map/ppermute | solution.py:267
  1388.6 19.9 %collective-permute-start.46 = (bf16[2,32,4096]{2,1,0:T(8,128)(2,1)S(1)}, bf16[2,32,4096]{2,1,0:T(8,128)(2,1)S(1)}, u32[]{:S(2)}, u32[]{:S(2)}) collective-permute-start(bf16[2,32,4096]{2,1,0:T(8,128)(2,1)S(1)} %fusion.98), channel_id=1, source_target_pairs={{0,2},{2,4},{4,6},{6,0},{1,3},{3,5},{5,7},{7,1},{8,10},{10,12},{12... | collective-permute-start | bytes 1572872 | tf_op jit(solution)/shard_map/ppermute | solution.py:267
  (98 other events, 2224.1 us)
Sparse Core Ops, SparseCore 0:
  91.1 79.5 all-gather.1

commit v2 on v1

v2 whole, which is shorter than its diff:
```python
from functools import partial
import math

import jax
import jax.numpy as jnp
from jax import lax
from jax.experimental import pallas as pl
from jax.experimental.pallas import tpu as pltpu
from jax.sharding import Mesh, PartitionSpec as P

HEADS = 16
HEAD = 64
EPSILON = 1e-05
SCALE = 1.0 / math.sqrt(HEAD)
AXES = ("y", "core", "z", "x")
NN = (((1,), (0,)), ((), ()))
NT = (((1,), (1,)), ((), ()))
TN = (((0,), (0,)), ((), ()))
LANES = 128
QUERIES = 128
REACH = 256
MASKED = -1e30
VMEM_LIMIT = 60 * 1024 * 1024
ANY = pl.BlockSpec(memory_space=pl.ANY)
SMEM = pl.BlockSpec(memory_space=pltpu.SMEM)


def dot(left, right, dims=NN):
    return lax.dot_general(left, right, dims, preferred_element_type=jnp.float32)


def params(limit=VMEM_LIMIT):
    return pltpu.CompilerParams(vmem_limit_bytes=limit)


def cost(flops, moved, special=0):
    return pl.CostEstimate(flops=int(flops), bytes_accessed=int(moved), transcendentals=int(special))


def ring(num):
    return [(place, (place + 1) % num) for place in range(num)]


class Grid:
    def __init__(self, sizes):
        self.sizes = dict(zip(AXES, sizes))
        self.total = math.prod(sizes)

    def coords(self):
        return {name: lax.axis_index(name) for name in AXES}

    def block(self, coords):
        place = 0
        for name in AXES:
            place = place * self.sizes[name] + coords[name]
        return place


def gather_pieces(grid, own, order):
    held = [own[None]]
    for name in order:
        held = [jnp.concatenate(held, 0) if len(held) > 1 else held[0]]
        for _ in range(grid.sizes[name] - 1):
            held.append(lax.ppermute(held[-1], name, ring(grid.sizes[name])))
    return held


def block_places(grid, coords, order):
    sizes = [grid.sizes[name] for name in order]
    places = []
    for slot in range(math.prod(sizes)):
        here = {}
        left = slot
        for name, size in zip(order, sizes):
            here[name] = lax.rem(coords[name] - left % size + size, size)
            left //= size
        places.append(grid.block(here))
    return jnp.stack(places).astype(jnp.int32)


class Gathered:
    def __init__(self, pieces, places):
        rows = pieces[0].shape[1]
        if rows % 16:
            blocks = jnp.concatenate(pieces, 0)
            placed = jnp.zeros_like(blocks).at[places].set(blocks)
            pieces = [placed.reshape(1, -1, blocks.shape[2])]
            places = jnp.zeros((1,), jnp.int32)
        self.pieces, self.places = list(pieces), places

    @property
    def count(self):
        return len(self.pieces)


def row_copies(places, pieces, first, target, column, width, sem):
    copies, number = [], 0
    for piece in pieces:
        blocks, rows, _ = piece.shape
        for slot in range(blocks):
            start = pl.multiple_of(places[number] * rows, rows)
            copies.append(
                pltpu.make_async_copy(
                    piece.at[slot, :, pl.ds(first, width)],
                    target.at[pl.ds(start, rows), pl.ds(column, width)],
                    sem,
                )
            )
            number += 1
    return copies


def scatter_stages(grid, coords, terms, axes, order, wire):
    axes = list(axes)
    for name in order:
        dim = axes.index(name)
        size = grid.sizes[name]
        arrived = None
        for step in range(size - 1):
            block = lax.rem(coords[name] + (2 * size - 1 - step), size)
            sent = sum(
                lax.dynamic_index_in_dim(term, block, dim, keepdims=False).astype(jnp.float32)
                for term in terms
            )
            if arrived is not None:
                sent = sent + arrived.astype(jnp.float32)
            arrived = lax.ppermute(sent.astype(wire), name, ring(size))
        terms = [
            lax.dynamic_index_in_dim(term, coords[name], dim, keepdims=False) for term in terms
        ] + [arrived]
        axes.remove(name)
    return sum(term.astype(jnp.float32) for term in terms)


def center_rows(rows):
    mean = jnp.mean(rows, axis=-1, keepdims=True)
    centred = rows - mean
    rate = lax.rsqrt(jnp.mean(centred * centred, axis=-1, keepdims=True) + EPSILON)
    return centred * rate, rate


def norm_pull(unit, rate, gain, cots):
    scaled = cots * gain
    return rate * (
        scaled
        - jnp.mean(scaled, axis=-1, keepdims=True)
        - unit * jnp.mean(scaled * unit, axis=-1, keepdims=True)
    )


def column_sum(values):
    return jnp.sum(values, axis=0, keepdims=True)


def gelu_parts(values):
    bell = jnp.exp(values * values * -0.5)
    t = 1.0 / (1.0 + jnp.abs(values) * (0.3275911 / math.sqrt(2.0)))
    series = t * (
        0.5 * 0.254829592
        + t
        * (
            0.5 * -0.284496736
            + t * (0.5 * 1.421413741 + t * (0.5 * -1.453152027 + t * (0.5 * 1.061405429)))
        )
    )
    tail = series * bell
    phi = jnp.where(values < 0.0, tail, 1.0 - tail)
    return values * phi, phi + values * bell * (1.0 / math.sqrt(2.0 * math.pi))


def project_kernel(counts, places_a, places_b, *refs):
    pieces_a, refs = refs[: counts[0]], refs[counts[0] :]
    pieces_b, refs = refs[: counts[1]], refs[counts[1] :]
    cells, gain, shift, bias, normed, qkv, weight, sem = refs
    width = cells.shape[1]
    copies = row_copies(places_a, pieces_a, 0, weight, 0, 2 * width, sem) + row_copies(
        places_b, pieces_b, 0, weight, 2 * width, width, sem
    )

    @pl.when(pl.program_id(0) == 0)
    def _():
        for copy in copies:
            copy.start()

    unit, _ = center_rows(cells[...].astype(jnp.float32))
    rows = (unit * gain[...] + shift[...]).astype(jnp.bfloat16)
    normed[...] = rows

    @pl.when(pl.program_id(0) == 0)
    def _():
        for copy in copies:
            copy.wait()

    for part in range(3):
        here = pl.ds(part * width, width)
        qkv[part] = (dot(rows, weight[:, here]) + bias[:, here]).astype(jnp.bfloat16)


def project(first, second, cells, gain, shift, bias, block=256):
    rows, width = cells.shape
    vector = pl.BlockSpec((1, width), lambda i: (0, 0))
    return pl.pallas_call(
        partial(project_kernel, (first.count, second.count)),
        grid=(rows // block,),
        in_specs=[SMEM, SMEM]
        + [ANY] * (first.count + second.count)
        + [
            pl.BlockSpec((block, width), lambda i: (i, 0)),
            vector,
            vector,
            pl.BlockSpec((1, 3 * width), lambda i: (0, 0)),
        ],
        out_specs=[
            pl.BlockSpec((block, width), lambda i: (i, 0)),
            pl.BlockSpec((3, block, width), lambda i: (0, i, 0)),
        ],
        out_shape=[
            jax.ShapeDtypeStruct((rows, width), jnp.bfloat16),
            jax.ShapeDtypeStruct((3, rows, width), jnp.bfloat16),
        ],
        scratch_shapes=[pltpu.VMEM((width, 3 * width), jnp.bfloat16), pltpu.SemaphoreType.DMA],
        compiler_params=params(),
        cost_estimate=cost(6 * rows * width * width, 10 * rows * width + 6 * width * width),
        name="project",
    )(
        first.places,
        second.places,
        *first.pieces,
        *second.pieces,
        cells,
        gain.reshape(1, -1),
        shift.reshape(1, -1),
        bias.reshape(1, -1),
    )


def key_range(first, rows):
    return max(0, first - REACH), min(rows, first + QUERIES + REACH)


def pair_rows(block, low):
    zero = jnp.zeros_like(block)
    return jnp.concatenate([jnp.where(low, block, zero), jnp.where(low, zero, block)], 0)


def twice(block, axis):
    return jnp.concatenate([block, block], axis)


def attend_kernel(ids_col, ids_row, live_row, qkv, mixed, log_sums, bias):
    rows = qkv.shape[1]

    @pl.when(pl.program_id(0) == 0)
    def _():
        for block, first in enumerate(range(0, rows, QUERIES)):
            start, stop = key_range(first, rows)
            shape = (QUERIES, stop - start)
            same = ids_col[first : first + QUERIES, :] == ids_row[:, start:stop]
            query_at = lax.broadcasted_iota(jnp.int32, shape, 0) + first
            key_at = lax.broadcasted_iota(jnp.int32, shape, 1) + start
            allowed = same & ((live_row[:, start:stop] == 1) | (query_at == key_at))
            bias[block, :, 0 : stop - start] = jnp.where(allowed, 0.0, MASKED)

    low = lax.broadcasted_iota(jnp.int32, (QUERIES, LANES), 1) < HEAD
    for block, first in enumerate(range(0, rows, QUERIES)):
        start, stop = key_range(first, rows)
        here = slice(first, first + QUERIES)
        query = pair_rows(qkv[0, here, :] * jnp.bfloat16(SCALE), low)
        scores = dot(query, qkv[1, start:stop, :], NT) + twice(bias[block, :, 0 : stop - start], 0)
        top = jnp.max(scores, axis=1, keepdims=True)
        expd = jnp.exp(scores - top)
        total = jnp.sum(expd, axis=1, keepdims=True)
        out = dot(expd.astype(jnp.bfloat16), qkv[2, start:stop, :]) / total
        mixed[here, :] = jnp.where(low, out[:QUERIES], out[QUERIES:]).astype(jnp.bfloat16)
        spread = jnp.broadcast_to(top + jnp.log(total), (2 * QUERIES, LANES)).T[0:1]
        log_sums[0, 0:1, here] = spread[:, :QUERIES]
        log_sums[0, 1:2, here] = spread[:, QUERIES:]


def attend(ids, live, qkv):
    _, rows, width = qkv.shape
    pairs = width // LANES
    whole = pl.BlockSpec((1, rows), lambda h: (0, 0))
    return pl.pallas_call(
        attend_kernel,
        grid=(pairs,),
        in_specs=[
            pl.BlockSpec((rows, 1), lambda h: (0, 0)),
            whole,
            whole,
            pl.BlockSpec((3, rows, LANES), lambda h: (0, 0, h)),
        ],
        out_specs=[
            pl.BlockSpec((rows, LANES), lambda h: (0, h)),
            pl.BlockSpec((1, 2, rows), lambda h: (h, 0, 0)),
        ],
        out_shape=[
            jax.ShapeDtypeStruct((rows, width), jnp.bfloat16),
            jax.ShapeDtypeStruct((pairs, 2, rows), jnp.float32),
        ],
        scratch_shapes=[
            pltpu.VMEM((rows // QUERIES, QUERIES, QUERIES + 2 * REACH), jnp.float32)
        ],
        compiler_params=params(),
        cost_estimate=cost(25 * 10**9, 8 * rows * width, 10**7),
        name="attend",
    )(ids.reshape(rows, 1), ids, live, qkv)


def attend_back_kernel(
    ids_col, ids_row, live_col, qkv, log_sums, d_mixed, d_qkv, sums, bias, d_key, d_value
):
    rows = qkv.shape[1]

    @pl.when(pl.program_id(0) == 0)
    def _():
        for block, first in enumerate(range(0, rows, QUERIES)):
            start, stop = key_range(first, rows)
            shape = (stop - start, QUERIES)
            same = ids_col[start:stop, :] == ids_row[:, first : first + QUERIES]
            query_at = lax.broadcasted_iota(jnp.int32, shape, 1) + first
            key_at = lax.broadcasted_iota(jnp.int32, shape, 0) + start
            allowed = same & ((live_col[start:stop, :] == 1) | (query_at == key_at))
            bias[block, 0 : stop - start, :] = jnp.where(allowed, 0.0, MASKED)

    d_key[...] = jnp.zeros_like(d_key)
    d_value[...] = jnp.zeros_like(d_value)
    low = lax.broadcasted_iota(jnp.int32, (QUERIES, LANES), 1) < HEAD
    query_sum = jnp.zeros((1, LANES), jnp.float32)
    for block, first in enumerate(range(0, rows, QUERIES)):
        start, stop = key_range(first, rows)
        here = slice(first, first + QUERIES)
        query = pair_rows(qkv[0, here, :] * jnp.bfloat16(SCALE), low)
        cot = pair_rows(d_mixed[here, :], low)
        keys, values = qkv[1, start:stop, :], qkv[2, start:stop, :]
        scores = dot(keys, query, NT) + twice(bias[block, 0 : stop - start, :], 1)
        ends = jnp.concatenate([log_sums[0, 0:1, here], log_sums[0, 1:2, here]], 1)
        probs = jnp.exp(scores - ends)
        weighted = probs * dot(values, cot, NT)
        d_scores = (weighted - probs * column_sum(weighted)).astype(jnp.bfloat16)
        d_value[start:stop, :] += dot(probs.astype(jnp.bfloat16), cot)
        d_key[start:stop, :] += dot(d_scores, query)
        both = dot(d_scores, keys, TN)
        d_query = (jnp.where(low, both[:QUERIES], both[QUERIES:]) * SCALE).astype(jnp.bfloat16)
        d_qkv[0, here, :] = d_query
        query_sum = query_sum + column_sum(d_query.astype(jnp.float32))
    d_qkv[1] = d_key[...].astype(jnp.bfloat16)
    value_low = d_value[...].astype(jnp.bfloat16)
    d_qkv[2] = value_low
    sums[0:1, :] = query_sum
    sums[1:2, :] = column_sum(value_low.astype(jnp.float32))


def attend_back(ids, live, qkv, log_sums, d_mixed):
    _, rows, width = qkv.shape
    pairs = width // LANES
    column = pl.BlockSpec((rows, 1), lambda h: (0, 0))
    triple = pl.BlockSpec((3, rows, LANES), lambda h: (0, 0, h))
    return pl.pallas_call(
        attend_back_kernel,
        grid=(pairs,),
        in_specs=[
            column,
            pl.BlockSpec((1, rows), lambda h: (0, 0)),
            column,
            triple,
            pl.BlockSpec((1, 2, rows), lambda h: (h, 0, 0)),
            pl.BlockSpec((rows, LANES), lambda h: (0, h)),
        ],
        out_specs=[triple, pl.BlockSpec((2, LANES), lambda h: (0, h))],
        out_shape=[
            jax.ShapeDtypeStruct(qkv.shape, jnp.bfloat16),
            jax.ShapeDtypeStruct((2, width), jnp.float32),
        ],
        scratch_shapes=[
            pltpu.VMEM((rows // QUERIES, QUERIES + 2 * REACH, QUERIES), jnp.float32),
            pltpu.VMEM((rows, LANES), jnp.float32),
            pltpu.VMEM((rows, LANES), jnp.float32),
        ],
        compiler_params=params(),
        cost_estimate=cost(38 * 10**9, 16 * rows * width, 10**7),
        name="attend_back",
    )(ids.reshape(rows, 1), ids, live.reshape(rows, 1), qkv, log_sums, d_mixed)


def feed_kernel(counts, chunk, places_out, places_up, places_down, *refs):
    pieces_out, refs = refs[: counts[0]], refs[counts[0] :]
    pieces_up, refs = refs[: counts[1]], refs[counts[1] :]
    pieces_down, refs = refs[: counts[2]], refs[counts[2] :]
    mixed, cells, out_grad, vectors, up_bias, refs = *refs[:5], refs[5:]
    normed, hidden, d_up, out_cells, d_inner, e_rows, d_mixed, sums, up_sums, refs = (
        *refs[:9],
        refs[9:],
    )
    w_out, w_up, w_down, slopes, sem_out, sem_up, sem_down = refs
    width, wide = w_up.shape
    out_copies = row_copies(places_out, pieces_out, width, w_out, 0, width, sem_out)
    up_copies = row_copies(places_up, pieces_up, 0, w_up, 0, wide, sem_up)
    down_copies = row_copies(places_down, pieces_down, 0, w_down, 0, width, sem_down)
    opening = pl.program_id(0) == 0

    @pl.when(opening)
    def _():
        for copy in out_copies + up_copies + down_copies:
            copy.start()
        sums[...] = jnp.zeros_like(sums)
        up_sums[...] = jnp.zeros_like(up_sums)
        for copy in out_copies:
            copy.wait()

    gain, shift = vectors[0:1, :], vectors[1:2, :]
    inner = cells[...].astype(jnp.float32) + dot(mixed[...], w_out[...]) + vectors[2:3, :]
    unit, rate = center_rows(inner)
    rows = (unit * gain + shift).astype(jnp.bfloat16)
    normed[...] = rows

    @pl.when(opening)
    def _():
        for copy in up_copies:
            copy.wait()

    for first in range(0, wide, chunk):
        here = slice(first, first + chunk)
        value, slope = gelu_parts(dot(rows, w_up[:, here]) + up_bias[:, here])
        hidden[:, here] = value.astype(jnp.bfloat16)
        slopes[:, here] = slope

    @pl.when(opening)
    def _():
        for copy in down_copies:
            copy.wait()

    layer_out = inner + dot(hidden[...], w_down[...]) + vectors[3:4, :]
    out_cells[...] = layer_out.astype(jnp.bfloat16)
    cot = out_grad[...]
    for first in range(0, wide, chunk):
        here = slice(first, first + chunk)
        slope = (dot(cot, w_down[here, :], NT) * slopes[:, here]).astype(jnp.bfloat16)
        d_up[:, here] = slope
        up_sums[:, here] += column_sum(slope.astype(jnp.float32))
    d_two = dot(d_up[...], w_up[...], NT)
    cot_wide = cot.astype(jnp.float32)
    pulled = cot_wide + norm_pull(unit, rate, gain, d_two)
    d_inner[...] = pulled
    low = pulled.astype(jnp.bfloat16)
    e_rows[...] = low
    d_mixed[...] = dot(low, w_out[...], NT).astype(jnp.bfloat16)
    sums[0:1, :] += column_sum(d_two * unit)
    sums[1:2, :] += column_sum(d_two)
    sums[2:3, :] += column_sum(low.astype(jnp.float32))
    sums[3:4, :] += column_sum(cot_wide)


def feed(out_w, up_w, down_w, mixed, cells, out_grad, vectors, up_bias, block=256, chunk=512):
    rows, width = cells.shape
    wide = up_bias.shape[0]
    narrow = pl.BlockSpec((block, width), lambda i: (i, 0))
    broad = pl.BlockSpec((block, wide), lambda i: (i, 0))
    low, full = jnp.bfloat16, jnp.float32
    struct = jax.ShapeDtypeStruct
    return pl.pallas_call(
        partial(feed_kernel, (out_w.count, up_w.count, down_w.count), chunk),
        grid=(rows // block,),
        in_specs=[SMEM] * 3
        + [ANY] * (out_w.count + up_w.count + down_w.count)
        + [
            narrow,
            narrow,
            narrow,
            pl.BlockSpec((4, width), lambda i: (0, 0)),
            pl.BlockSpec((1, wide), lambda i: (0, 0)),
        ],
        out_specs=[
            narrow,
            broad,
            broad,
            narrow,
            narrow,
            narrow,
            narrow,
            pl.BlockSpec((4, width), lambda i: (0, 0)),
            pl.BlockSpec((1, wide), lambda i: (0, 0)),
        ],
        out_shape=[
            struct((rows, width), low),
            struct((rows, wide), low),
            struct((rows, wide), low),
            struct((rows, width), low),
            struct((rows, width), full),
            struct((rows, width), low),
            struct((rows, width), low),
            struct((4, width), full),
            struct((1, wide), full),
        ],
        scratch_shapes=[
            pltpu.VMEM((width, width), low),
            pltpu.VMEM((width, wide), low),
            pltpu.VMEM((wide, width), low),
            pltpu.VMEM((block, wide), full),
            pltpu.SemaphoreType.DMA,
            pltpu.SemaphoreType.DMA,
            pltpu.SemaphoreType.DMA,
        ],
        compiler_params=params(),
        cost_estimate=cost(
            rows * width * (8 * wide + 4 * width), rows * (4 * wide + 20 * width) + 18 * 2**20, 10**7
        ),
        name="feed",
    )(
        out_w.places,
        up_w.places,
        down_w.places,
        *out_w.pieces,
        *up_w.pieces,
        *down_w.pieces,
        mixed,
        cells,
        out_grad,
        vectors,
        up_bias.reshape(1, -1),
    )


def grad_kernel(_, left, right, out):
    cots = right[...].reshape(right.shape[-2:])
    out[0] = dot(left[...], cots, TN).astype(out.dtype)


def half_grad(core, left, right, columns, outer, block=256, chunk=512):
    rows, width = left.shape
    per_outer = width // (2 * outer)
    block = min(block, per_outer)
    steps = per_outer // block
    first, span = columns
    depth = right.shape[-1] // chunk
    if right.ndim == 3:
        right_spec = pl.BlockSpec(
            (1, rows, chunk),
            lambda n, y, m, c: ((first // chunk + n) // depth, 0, (first // chunk + n) % depth),
        )
    else:
        right_spec = pl.BlockSpec((rows, chunk), lambda n, y, m, c: (0, first // chunk + n))
    return pl.pallas_call(
        grad_kernel,
        grid_spec=pltpu.PrefetchScalarGridSpec(
            num_scalar_prefetch=1,
            grid=(span // chunk, outer, steps),
            in_specs=[
                pl.BlockSpec((rows, block), lambda n, y, m, c: (0, (y * 2 + c[0]) * steps + m)),
                right_spec,
            ],
            out_specs=pl.BlockSpec((1, block, chunk), lambda n, y, m, c: (y, m, n)),
        ),
        out_shape=jax.ShapeDtypeStruct((outer, per_outer, span), jnp.bfloat16),
        compiler_params=params(),
        cost_estimate=cost(rows * width * span, rows * (width + 2 * span) + width * span),
        name="half_grad",
    )(core.reshape(1), left, right)


def weight_grad(grid, coords, left, right, columns):
    outer = grid.sizes["y"]

    def part(core):
        product = half_grad(core, left, right, columns, outer)
        return product.reshape(outer, grid.sizes["z"], grid.sizes["x"], -1, columns[1])

    sent = part(1 - coords["core"])
    arrived = lax.ppermute(sent, "core", ring(2))
    return [part(coords["core"]), arrived]


def cells_kernel(counts, places_a, places_b, *refs):
    pieces_a, refs = refs[: counts[0]], refs[counts[0] :]
    pieces_b, refs = refs[: counts[1]], refs[counts[1] :]
    d_qkv, cells, d_inner, gain, cells_grad, sums, weight, sem = refs
    width = cells.shape[1]
    copies = row_copies(places_a, pieces_a, 0, weight, 0, 2 * width, sem) + row_copies(
        places_b, pieces_b, 0, weight, 2 * width, width, sem
    )
    opening = pl.program_id(0) == 0

    @pl.when(opening)
    def _():
        for copy in copies:
            copy.start()
        sums[...] = jnp.zeros_like(sums)

    unit, rate = center_rows(cells[...].astype(jnp.float32))

    @pl.when(opening)
    def _():
        for copy in copies:
            copy.wait()

    d_one = sum(
        dot(d_qkv[part], weight[:, pl.ds(part * width, width)], NT) for part in range(3)
    )
    cells_grad[...] = (d_inner[...] + norm_pull(unit, rate, gain[...], d_one)).astype(jnp.bfloat16)
    sums[0:1, :] += column_sum(d_one * unit)
    sums[1:2, :] += column_sum(d_one)


def cells_back(first, second, d_qkv, cells, d_inner, gain, block=256):
    rows, width = cells.shape
    narrow = pl.BlockSpec((block, width), lambda i: (i, 0))
    return pl.pallas_call(
        partial(cells_kernel, (first.count, second.count)),
        grid=(rows // block,),
        in_specs=[SMEM, SMEM]
        + [ANY] * (first.count + second.count)
        + [
            pl.BlockSpec((3, block, width), lambda i: (0, i, 0)),
            narrow,
            narrow,
            pl.BlockSpec((1, width), lambda i: (0, 0)),
        ],
        out_specs=[narrow, pl.BlockSpec((2, width), lambda i: (0, 0))],
        out_shape=[
            jax.ShapeDtypeStruct((rows, width), jnp.bfloat16),
            jax.ShapeDtypeStruct((2, width), jnp.float32),
        ],
        scratch_shapes=[pltpu.VMEM((width, 3 * width), jnp.bfloat16), pltpu.SemaphoreType.DMA],
        compiler_params=params(),
        cost_estimate=cost(6 * rows * width * width, 14 * rows * width + 6 * width * width),
        name="cells_back",
    )(
        first.places,
        second.places,
        *first.pieces,
        *second.pieces,
        d_qkv,
        cells,
        d_inner,
        gain.reshape(1, -1),
    )


def local(
    grid,
    cells,
    segment_ids,
    valid,
    norm1_gain,
    norm1_bias,
    qkv_weight,
    qv_bias,
    out_weight,
    out_bias,
    norm2_gain,
    norm2_bias,
    up_weight,
    up_bias,
    down_weight,
    down_bias,
    out_grad,
):
    width = cells.shape[1]
    wide = up_weight.shape[1]
    coords = grid.coords()
    own_rows = qkv_weight.shape[0]
    order_a = ("x", "z", "y", "core")
    order_b = ("y", "z", "x", "core")
    places_a = block_places(grid, coords, order_a)
    places_b = block_places(grid, coords, order_b)
    vectors = (
        norm1_gain,
        norm1_bias,
        qv_bias,
        out_bias,
        norm2_gain,
        norm2_bias,
        up_bias,
        down_bias,
    )
    packed = jnp.concatenate(vectors)
    packed_size = packed.shape[0]
    packed = jnp.pad(packed, (0, own_rows * LANES - packed_size)).reshape(own_rows, LANES)
    w_up = lax.all_gather(up_weight, AXES, axis=0, tiled=True)
    pieces_a = gather_pieces(grid, qkv_weight[:, : 2 * width], order_a)
    pieces_b = gather_pieces(
        grid, jnp.concatenate([qkv_weight[:, 2 * width :], out_weight, packed], 1), order_b
    )
    queries_keys = Gathered(pieces_a, places_a)
    values_out = Gathered(pieces_b, places_b)
    down_own, _ = lax.optimization_barrier((down_weight, pieces_b[-1]))
    down_all = Gathered(gather_pieces(grid, down_own, order_a), places_a)
    up_all = Gathered([w_up[None]], jnp.zeros((1,), jnp.int32))

    arrived = jnp.concatenate(pieces_b, 0)[:, :, 2 * width :].reshape(grid.total, -1)
    arrived = jnp.zeros_like(arrived).at[places_b].set(arrived)[:, :packed_size]
    spread, first = [], 0
    for vector in vectors:
        size = vector.shape[0]
        spread.append(arrived[:, first : first + size].reshape(-1).astype(jnp.float32))
        first += size
    gain_one, shift_one, b_qv, b_out, gain_two, shift_two, b_up, b_down = spread

    qkv_bias = jnp.concatenate([b_qv[:width], jnp.zeros_like(b_out), b_qv[width:]])
    normed, qkv = project(queries_keys, values_out, cells, gain_one, shift_one, qkv_bias)
    mixed, log_sums = attend(segment_ids, valid, qkv)
    normed_two, hidden, d_up, out_cells, d_inner, e_rows, d_mixed, sums, up_sums = feed(
        values_out,
        up_all,
        down_all,
        mixed,
        cells,
        out_grad,
        jnp.stack([gain_two, shift_two, b_out, b_down]),
        b_up,
    )

    def total(terms, order):
        return scatter_stages(grid, coords, terms, ("y", "z", "x"), order, jnp.bfloat16)

    down_total = total(weight_grad(grid, coords, hidden, out_grad, (0, width)), ("x", "z", "y"))
    up_total = total(weight_grad(grid, coords, normed_two, d_up, (0, wide)), ("y", "z", "x"))
    out_total = total(weight_grad(grid, coords, mixed, e_rows, (0, width)), ("x", "z", "y"))
    d_qkv, qv_sums = attend_back(segment_ids, valid, qkv, log_sums, d_mixed)
    half = 3 * width // 2
    qkv_total = jnp.concatenate(
        [
            total(weight_grad(grid, coords, normed, d_qkv, (0, half)), ("x", "z", "y")),
            total(weight_grad(grid, coords, normed, d_qkv, (half, half)), ("y", "z", "x")),
        ],
        1,
    )
    cells_grad, one_sums = cells_back(queries_keys, values_out, d_qkv, cells, d_inner, gain_one)

    vector_grads = (
        one_sums[0],
        one_sums[1],
        qv_sums,
        sums[2],
        sums[0],
        sums[1],
        up_sums,
        sums[3],
    )
    sizes = [grid.sizes[name] for name in AXES]
    stacked = jnp.concatenate([grad.reshape(*sizes, -1) for grad in vector_grads], -1)
    summed = scatter_stages(
        grid, coords, [stacked], AXES, ("core", "x", "z", "y"), jnp.float32
    )
    parts, first = [], 0
    for vector in vectors:
        parts.append(summed[first : first + vector.shape[0]])
        first += vector.shape[0]
    return (
        out_cells,
        cells_grad,
        parts[0],
        parts[1],
        qkv_total,
        parts[2],
        out_total,
        parts[3],
        parts[4],
        parts[5],
        up_total,
        parts[6],
        down_total,
        parts[7],
    )


def solution(mesh):
    outer, inner_size = mesh.devices.shape
    sizes = (outer // 2, 2, inner_size // 2, 2)
    fine = Mesh(mesh.devices.reshape(sizes), AXES)
    rows, vector = P(AXES, None), P(AXES)
    return jax.shard_map(
        partial(local, Grid(sizes)),
        mesh=fine,
        in_specs=(
            rows,
            rows,
            rows,
            vector,
            vector,
            rows,
            vector,
            rows,
            vector,
            vector,
            vector,
            rows,
            vector,
            rows,
            vector,
            rows,
        ),
        out_specs=(
            rows,
            rows,
            vector,
            vector,
            rows,
            vector,
            rows,
            vector,
            vector,
            vector,
            rows,
            vector,
            rows,
            vector,
        ),
        check_vma=False,
    )
```

time: 1440 us -> 710 us (0.49)
  matrix products: 306 us -> 0 us
  Pallas kernels: 520 us -> 267 us
  local copies, waits for them, and re-layouts: 191 us -> 35.8 us
  other arithmetic: 134 us -> 38.5 us
  waiting for transfers between devices: 229 us -> 304 us
    dot_general x74 -> x0, matrix products: 306 us -> none  [the longest x4 54.9 us: times_right(): lax.dot_general(left_mat, right_mat, (((1,), (1,)), ((), ())), preferred_...]
    pallas_call x2 -> x15, Pallas kernels: 520 us -> 267 us  [the longest x10 105 us: half_grad(): pl.pallas_call(grad_kernel, grid_spec=pltpu.PrefetchScalarGridSpec(num_sc...]
    ppermute x18, waiting for transfers between devices: 108 us -> 190 us  [gather_pieces(): held.append(lax.ppermute(held[-1], name, ring(grid.sizes[name])))]
    unnamed x167 -> x43, local copies, waits for them, and re-layouts: 67.9 us -> 11 us
    dynamic_slice x15 -> x0, local copies, waits for them, and re-layouts: 41 us -> none  [the longest x3 27.3 us: part(): chosen = lax.dynamic_index_in_dim(split, core, 2, keepdims=False)]
    reduce_sum x18 -> x0, other arithmetic: 38.8 us -> none  [the longest x8 18.7 us: attend_forward(): row_total = jnp.sum(expd, axis=-1, keepdims=True)]
    convert_element_type x14 -> x2, other arithmetic: 35.9 us -> 0.75 us  [local(): arrived[:, first:first + size].reshape(-1).astype(jnp.float32)]
    reshape x6 -> x3, local copies, waits for them, and re-layouts: 26 us -> 2.06 us  [the longest x1 1.03 us: attend(): ids.reshape(rows, 1)]
  transfers between devices with their start and end apart: 55 -> 55, of which waited for: 32 -> 34; matrix products, arithmetic and copies ran while one was open for 21% -> 10% of each run, Pallas kernels for 36% -> 12%
where the time goes in v2:
time: 710 us; the launch traced here: 699 us
  waiting for transfers between devices  304 us (43%)
  Pallas kernels  267 us (38%)
  starting transfers between devices  39 us (5%)
  other arithmetic  38.5 us (5%)
  local copies, waits for them, and re-layouts  35.8 us (5%)
  between operations  15.1 us (2%)
    ppermute x18, waiting for transfers between devices, gather_pieces(): held.append(lax.ppermute(held[-1], name, ring(grid.sizes[name])))  190 us
    ppermute x31, waiting for transfers between devices, scatter_stages(): arrived = lax.ppermute(sent.astype(wire), name, ring(size))  114 us
    pallas_call x10, Pallas kernels, half_grad(): pl.pallas_call(grad_kernel, grid_spec=pltpu.PrefetchScalarGridSpec(num_sc...  105 us
    pallas_call x1, Pallas kernels, feed(): pl.pallas_call(partial(feed_kernel, (out_w.count, up_w.count, down_w.coun...  67.1 us
    pallas_call x1, Pallas kernels, attend_back(): pl.pallas_call(attend_back_kernel, grid=(pairs,), in_specs=[column, pl.Bl...  37.8 us
    pallas_call x1, Pallas kernels, attend(): pl.pallas_call(attend_kernel, grid=(pairs,), in_specs=[pl.BlockSpec((rows...  27.9 us
    convert_element_type x25, other arithmetic, scatter_stages(): arrived = lax.ppermute(sent.astype(wire), name, ring(size))  26.7 us
    ppermute x18, starting transfers between devices, gather_pieces(): held.append(lax.ppermute(held[-1], name, ring(grid.sizes[name])))  20.5 us
  transfers between devices with their start and end apart: 55, of which 34 were waited for; matrix products, arithmetic and copies ran while one was open for 10% of the time, Pallas kernels for 12%

profile of v2, /device:TPU:0, one launch (start us, length us, event | category | flops | bytes accessed | tf_op | source)
XLA Modules:
  0.0 699.3 jit_solution(4896084164661680986)
XLA Ops:
  8.8 5.4 concatenate.71
  24.3 12.4 %collective-permute-done.1 = bf16[2,32,2176]{2,1,0:T(8,128)(2,1)S(1)} collective-permute-done((bf16[2,32,2176]{2,1,0:T(8,128)(2,1)S(1)}, bf16[2,32,2176]{2,1,0:T(8,128)(2,1)S(1)}, u32[]{:S(2)}, u32[]{:S(2)}) %collective-permute-start.1) | collective-permute-done | bytes 278560 | tf_op jit(solution)/shard_map/ppermute | solution.py:64
  37.5 7.6 %collective-permute-done.2 = bf16[2,32,2176]{2,1,0:T(8,128)(2,1)S(1)} collective-permute-done((bf16[2,32,2176]{2,1,0:T(8,128)(2,1)S(1)}, bf16[2,32,2176]{2,1,0:T(8,128)(2,1)S(1)}, u32[]{:S(2)}, u32[]{:S(2)}) %collective-permute-start.2) | collective-permute-done | bytes 278560 | tf_op jit(solution)/shard_map/ppermute | solution.py:64
  45.9 13.6 %collective-permute-done.3 = bf16[2,32,2176]{2,1,0:T(8,128)(2,1)S(1)} collective-permute-done((bf16[2,32,2176]{2,1,0:T(8,128)(2,1)S(1)}, bf16[2,32,2176]{2,1,0:T(8,128)(2,1)S(1)}, u32[]{:S(2)}, u32[]{:S(2)}) %collective-permute-start.3) | collective-permute-done | bytes 278560 | tf_op jit(solution)/shard_map/ppermute | solution.py:64
  61.7 31.3 %collective-permute-done.4 = bf16[8,32,2176]{2,1,0:T(8,128)(2,1)S(1)} collective-permute-done((bf16[8,32,2176]{2,1,0:T(8,128)(2,1)S(1)}, bf16[8,32,2176]{2,1,0:T(8,128)(2,1)S(1)}, u32[]{:S(2)}, u32[]{:S(2)}) %collective-permute-start.4) | collective-permute-done | bytes 1114144 | tf_op jit(solution)/shard_map/ppermute | solution.py:64
  98.8 8.1 %collective-permute-done.6 = bf16[1,128,1024]{2,1,0:T(8,128)(2,1)S(1)} collective-permute-done((bf16[1,128,1024]{2,1,0:T(8,128)(2,1)S(1)}, bf16[1,128,1024]{2,1,0:T(8,128)(2,1)S(1)}, u32[]{:S(2)}, u32[]{:S(2)}) %collective-permute-start.6) | collective-permute-done | bytes 262176 | tf_op jit(solution)/shard_map/ppermute | solution.py:64
  120.4 8.6 %collective-permute-done.7 = bf16[2,128,1024]{2,1,0:T(8,128)(2,1)S(1)} collective-permute-done((bf16[2,128,1024]{2,1,0:T(8,128)(2,1)S(1)}, bf16[2,128,1024]{2,1,0:T(8,128)(2,1)S(1)}, u32[]{:S(2)}, u32[]{:S(2)}) %collective-permute-start.7) | collective-permute-done | bytes 524320 | tf_op jit(solution)/shard_map/ppermute | solution.py:64
  136.1 14.0 %collective-permute-done.14 = bf16[2,32,2048]{2,1,0:T(8,128)(2,1)S(1)} collective-permute-done((bf16[2,32,2048]{2,1,0:T(8,128)(2,1)S(1)}, bf16[2,32,2048]{2,1,0:T(8,128)(2,1)S(1)}, u32[]{:S(2)}, u32[]{:S(2)}) %collective-permute-start.14) | collective-permute-done | bytes 262176 | tf_op jit(solution)/shard_map/ppermute | solution.py:64
  155.1 14.8 %collective-permute-done.9 = bf16[2,128,1024]{2,1,0:T(8,128)(2,1)S(1)} collective-permute-done((bf16[2,128,1024]{2,1,0:T(8,128)(2,1)S(1)}, bf16[2,128,1024]{2,1,0:T(8,128)(2,1)S(1)}, u32[]{:S(2)}, u32[]{:S(2)}) %collective-permute-start.9) | collective-permute-done | bytes 524320 | tf_op jit(solution)/shard_map/ppermute | solution.py:64
  174.6 64.4 %collective-permute-done.16 = bf16[8,32,2048]{2,1,0:T(8,128)(2,1)S(1)} collective-permute-done((bf16[8,32,2048]{2,1,0:T(8,128)(2,1)S(1)}, bf16[8,32,2048]{2,1,0:T(8,128)(2,1)S(1)}, u32[]{:S(2)}, u32[]{:S(2)}) %collective-permute-start.16) | collective-permute-done | bytes 1048608 | tf_op jit(solution)/shard_map/ppermute | solution.py:64
  254.7 13.7 %project.1 = (bf16[1024,1024]{1,0:T(8,128)(2,1)}, bf16[3,1024,1024]{2,1,0:T(8,128)(2,1)}) custom-call(s32[32]{0:T(128)} %stack.242.places_a.places_down, s32[32]{0:T(128)} %stack.241.places_b.places_out, bf16[16,32,2048]{2,1,0:T(8,128)(2,1)} %constant_dynamic-update-slice_fusion.27.refs_0_, bf16[16,32,2048]{2,1,0:T(8,128)(2,1)} %collective-permute-done.17.refs_1_, ...), custom_call_target="tpu_custom_call" | custom-call | flops 6442450944 | bytes 16777216 | tf_op jit(solution)/shard_map/project/pallas_call | solution.py:202
  268.4 27.9 %attend.1 = (bf16[1024,1024]{1,0:T(8,128)(2,1)}, f32[8,2,1024]{2,1,0:T(2,128)}) custom-call(s32[1024,1]{1,0:T(8,128)} %copy.51.ids_col, s32[1,1024]{1,0:T(1,128)} %ids_row.3, s32[1,1024]{1,0:T(1,128)} %live_row.1, bf16[3,1024,1024]{2,1,0:T(8,128)(2,1)} %get-tuple-element.33.qkv), custom_call_target="tpu_custom_call" | custom-call | flops 24999999488 | bytes 8388608 | tf_op jit(solution)/shard_map/attend/pallas_call | solution.py:284
  296.3 67.1 %feed.1 = (bf16[1024,1024]{1,0:T(8,128)(2,1)}, bf16[1024,4096]{1,0:T(8,128)(2,1)}, bf16[1024,4096]{1,0:T(8,128)(2,1)}, bf16[1024,1024]{1,0:T(8,128)(2,1)}, f32[1...) custom-call(s32[32]{0:T(128)} %stack.241.places_b.places_out, ...), custom_call_target="tpu_custom_call" | custom-call | flops 38654705664 | bytes 56623104 | tf_op jit(solution)/shard_map/feed/pallas_call | solution.py:461
  363.5 15.1 %half_grad.19 = bf16[2,1024,1024]{2,1,0:T(8,128)(2,1)} custom-call(s32[1]{0:T(128)} %bitcast.78._, bf16[1024,4096]{1,0:T(8,128)(2,1)} %get-tuple-element.49.left, bf16[1024,1024]{1,0:T(8,128)(2,1)} %right.3), custom_call_target="tpu_custom_call" | custom-call | flops 4294967296 | bytes 10485760 | tf_op jit(solution)/shard_map/half_grad/pallas_call | solution.py:543
  378.6 15.1 %half_grad.18 = bf16[2,1024,1024]{2,1,0:T(8,128)(2,1)} custom-call(s32[1]{0:T(128)} %bitcast.76._, bf16[1024,4096]{1,0:T(8,128)(2,1)} %get-tuple-element.49.left, bf16[1024,1024]{1,0:T(8,128)(2,1)} %right.3), custom_call_target="tpu_custom_call" | custom-call | flops 4294967296 | bytes 10485760 | tf_op jit(solution)/shard_map/half_grad/pallas_call | solution.py:543
  393.7 17.5 %half_grad.16 = bf16[2,256,4096]{2,1,0:T(8,128)(2,1)} custom-call(s32[1]{0:T(128)} %bitcast.76._, bf16[1024,1024]{1,0:T(8,128)(2,1)} %get-tuple-element.47.left, bf16[1024,4096]{1,0:T(8,128)(2,1)} %get-tuple-element.48.right), custom_call_target="tpu_custom_call" | custom-call | flops 4294967296 | bytes 13631488 | tf_op jit(solution)/shard_map/half_grad/pallas_call | solution.py:543
  411.2 17.5 %half_grad.17 = bf16[2,256,4096]{2,1,0:T(8,128)(2,1)} custom-call(s32[1]{0:T(128)} %bitcast.78._, bf16[1024,1024]{1,0:T(8,128)(2,1)} %get-tuple-element.47.left, bf16[1024,4096]{1,0:T(8,128)(2,1)} %get-tuple-element.48.right), custom_call_target="tpu_custom_call" | custom-call | flops 4294967296 | bytes 13631488 | tf_op jit(solution)/shard_map/half_grad/pallas_call | solution.py:543
  428.8 37.8 %attend_back.1 = (bf16[3,1024,1024]{2,1,0:T(8,128)(2,1)}, f32[2,1024]{1,0:T(2,128)}) custom-call(s32[1024,1]{1,0:T(8,128)} %copy.51.ids_col, s32[1,1024]{1,0:T(1,128)} %ids_row.3, s32[1024,1]{1,0:T(8,128)} %copy.53.live_col, bf16[3,1024,1024]{2,1,0:T(8,128)(2,1)} %get-tuple-element.33.qkv, f32[8,2,1024]{2,1,0:T(2,128)} %get-tuple-element.36.log_sums, ...), custom_call_target="tpu_custom_call" | custom-call | flops 38000001024 | bytes 16777216 | tf_op jit(solution)/shard_map/attend_back/pallas_call | solution.py:359
  466.6 7.3 %half_grad.10 = bf16[2,256,1536]{2,1,0:T(8,128)(2,1)} custom-call(s32[1]{0:T(128)} %bitcast.76._, bf16[1024,1024]{1,0:T(8,128)(2,1)} %get-tuple-element.45.left, bf16[3,1024,1024]{2,1,0:T(8,128)(2,1)} %get-tuple-element.38.refs_4_.right), custom_call_target="tpu_custom_call" | custom-call | flops 1610612736 | bytes 5767168 | tf_op jit(solution)/shard_map/half_grad/pallas_call | solution.py:543
  473.9 7.2 %half_grad.11 = bf16[2,256,1536]{2,1,0:T(8,128)(2,1)} custom-call(s32[1]{0:T(128)} %bitcast.78._, bf16[1024,1024]{1,0:T(8,128)(2,1)} %get-tuple-element.45.left, bf16[3,1024,1024]{2,1,0:T(8,128)(2,1)} %get-tuple-element.38.refs_4_.right), custom_call_target="tpu_custom_call" | custom-call | flops 1610612736 | bytes 5767168 | tf_op jit(solution)/shard_map/half_grad/pallas_call | solution.py:543
  487.2 15.5 %cells_back.1 = (bf16[1024,1024]{1,0:T(8,128)(2,1)}, f32[2,1024]{1,0:T(2,128)}) custom-call(s32[32]{0:T(128)} %stack.242.places_a.places_down, s32[32]{0:T(128)} %stack.241.places_b.places_out, bf16[16,32,2048]{2,1,0:T(8,128)(2,1)} %constant_dynamic-update-slice_fusion.27.refs_0_, bf16[16,32,2048]{2,1,0:T(8,128)(2,1)} %collective-permute-done.17.refs_1_, ...), custom_call_target="tpu_custom_call" | custom-call | flops 6442450944 | bytes 20971520 | tf_op jit(solution)/shard_map/cells_back/pallas_call | solution.py:607
  504.6 7.3 %half_grad.12 = bf16[2,256,1536]{2,1,0:T(8,128)(2,1)} custom-call(s32[1]{0:T(128)} %bitcast.76._, bf16[1024,1024]{1,0:T(8,128)(2,1)} %get-tuple-element.45.left, bf16[3,1024,1024]{2,1,0:T(8,128)(2,1)} %get-tuple-element.38.refs_4_.right), custom_call_target="tpu_custom_call" | custom-call | flops 1610612736 | bytes 5767168 | tf_op jit(solution)/shard_map/half_grad/pallas_call | solution.py:543
  526.9 7.4 %half_grad.13 = bf16[2,256,1536]{2,1,0:T(8,128)(2,1)} custom-call(s32[1]{0:T(128)} %bitcast.78._, bf16[1024,1024]{1,0:T(8,128)(2,1)} %get-tuple-element.45.left, bf16[3,1024,1024]{2,1,0:T(8,128)(2,1)} %get-tuple-element.38.refs_4_.right), custom_call_target="tpu_custom_call" | custom-call | flops 1610612736 | bytes 5767168 | tf_op jit(solution)/shard_map/half_grad/pallas_call | solution.py:543
  555.9 6.1 collective-permute-done.40
  577.8 7.4 %collective-permute-done.31 = bf16[4,2,32,1536]{3,2,1,0:T(8,128)(2,1)S(1)} collective-permute-done((bf16[4,2,32,1536]{3,2,1,0:T(8,128)(2,1)S(1)}, bf16[4,2,32,1536]{3,2,1,0:T(8,128)(2,1)S(1)}, u32[]{:S(2)}, u32[]{:S(2)}) %collective-permute-start.31) | collective-permute-done | bytes 786464 | tf_op jit(solution)/shard_map/ppermute | solution.py:127
  586.4 8.1 %collective-permute-done.32 = bf16[2,32,1536]{2,1,0:T(8,128)(2,1)S(1)} collective-permute-done((bf16[2,32,1536]{2,1,0:T(8,128)(2,1)S(1)}, bf16[2,32,1536]{2,1,0:T(8,128)(2,1)S(1)}, u32[]{:S(2)}, u32[]{:S(2)}) %collective-permute-start.32) | collective-permute-done | bytes 196640 | tf_op jit(solution)/shard_map/ppermute | solution.py:127
  602.3 11.7 %collective-permute-done.49 = bf16[2,4,128,1024]{3,2,1,0:T(8,128)(2,1)S(1)} collective-permute-done((bf16[2,4,128,1024]{3,2,1,0:T(8,128)(2,1)S(1)}, bf16[2,4,128,1024]{3,2,1,0:T(8,128)(2,1)S(1)}, u32[]{:S(2)}, u32[]{:S(2)}) %collective-permute-start.49) | collective-permute-done | bytes 2097184 | tf_op jit(solution)/shard_map/ppermute | solution.py:127
  615.5 9.5 %collective-permute-done.43 = bf16[4,2,32,4096]{3,2,1,0:T(8,128)(2,1)S(1)} collective-permute-done((bf16[4,2,32,4096]{3,2,1,0:T(8,128)(2,1)S(1)}, bf16[4,2,32,4096]{3,2,1,0:T(8,128)(2,1)S(1)}, u32[]{:S(2)}, u32[]{:S(2)}) %collective-permute-start.43) | collective-permute-done | bytes 2097184 | tf_op jit(solution)/shard_map/ppermute | solution.py:127
  630.8 12.1 %collective-permute-done.44 = bf16[2,32,4096]{2,1,0:T(8,128)(2,1)S(1)} collective-permute-done((bf16[2,32,4096]{2,1,0:T(8,128)(2,1)S(1)}, bf16[2,32,4096]{2,1,0:T(8,128)(2,1)S(1)}, u32[]{:S(2)}, u32[]{:S(2)}) %collective-permute-start.44) | collective-permute-done | bytes 524320 | tf_op jit(solution)/shard_map/ppermute | solution.py:127
  645.3 8.9 %collective-permute-done.51 = bf16[2,128,1024]{2,1,0:T(8,128)(2,1)S(1)} collective-permute-done((bf16[2,128,1024]{2,1,0:T(8,128)(2,1)S(1)}, bf16[2,128,1024]{2,1,0:T(8,128)(2,1)S(1)}, u32[]{:S(2)}, u32[]{:S(2)}) %collective-permute-start.51) | collective-permute-done | bytes 524320 | tf_op jit(solution)/shard_map/ppermute | solution.py:127
  655.6 9.8 %collective-permute-done.45 = bf16[2,32,4096]{2,1,0:T(8,128)(2,1)S(1)} collective-permute-done((bf16[2,32,4096]{2,1,0:T(8,128)(2,1)S(1)}, bf16[2,32,4096]{2,1,0:T(8,128)(2,1)S(1)}, u32[]{:S(2)}, u32[]{:S(2)}) %collective-permute-start.45) | collective-permute-done | bytes 524320 | tf_op jit(solution)/shard_map/ppermute | solution.py:127
  666.9 9.8 %collective-permute-done.52 = bf16[2,128,1024]{2,1,0:T(8,128)(2,1)S(1)} collective-permute-done((bf16[2,128,1024]{2,1,0:T(8,128)(2,1)S(1)}, bf16[2,128,1024]{2,1,0:T(8,128)(2,1)S(1)}, u32[]{:S(2)}, u32[]{:S(2)}) %collective-permute-start.52) | collective-permute-done | bytes 524320 | tf_op jit(solution)/shard_map/ppermute | solution.py:127
  (234 shorter events, 164.1 us)
Async XLA Ops:
  7.2 289.1 %all-gather.2.cloned.1.call-start = ((), (), s32[]{:S(2)}) async-start(), calls=%async_computation | async-start | bytes 8650752 | tf_op jit(solution)/shard_map/all_gather | solution.py:679
  21.8 15.0 %collective-permute-start.1 = (bf16[2,32,2176]{2,1,0:T(8,128)(2,1)S(1)}, bf16[2,32,2176]{2,1,0:T(8,128)(2,1)S(1)}, u32[]{:S(2)}, u32[]{:S(2)}) collective-permute-start(bf16[2,32,2176]{2,1,0:T(8,128)(2,1)S(1)} %pad_maximum_fusion.2), channel_id=1, source_target_pairs={{0,2},{2,4},{4,6},{6,0},{1,3},{3,5},{5,7},{7,1},{8,10},{10,12},{12... | collective-permute-start | bytes 835592 | tf_op jit(solution)/shard_map/ppermute | solution.py:64
  60.2 32.8 %collective-permute-start.4 = (bf16[8,32,2176]{2,1,0:T(8,128)(2,1)S(1)}, bf16[8,32,2176]{2,1,0:T(8,128)(2,1)S(1)}, u32[]{:S(2)}, u32[]{:S(2)}) collective-permute-start(bf16[8,32,2176]{2,1,0:T(8,128)(2,1)S(1)} %get-tuple-element.74), channel_id=1, source_target_pairs={{0,1},{1,0},{2,3},{3,2},{4,5},{5,4},{6,7},{7,6},{8,9},{9,8},{10,11... | collective-permute-start | bytes 3342344 | tf_op jit(solution)/shard_map/ppermute | solution.py:64
  106.9 22.0 %collective-permute-start.7 = (bf16[2,128,1024]{2,1,0:T(8,128)(2,1)S(1)}, bf16[2,128,1024]{2,1,0:T(8,128)(2,1)S(1)}, u32[]{:S(2)}, u32[]{:S(2)}) collective-permute-start(bf16[2,128,1024]{2,1,0:T(8,128)(2,1)S(1)} %pad_maximum_fusion), channel_id=1, source_target_pairs={{0,2},{2,4},{4,6},{6,0},{1,3},{3,5},{5,7},{7,1},{8,10},{10,12},{12... | collective-permute-start | bytes 1572872 | tf_op jit(solution)/shard_map/ppermute | solution.py:64
  116.5 18.1 %collective-permute-start.13 = (bf16[2,32,2048]{2,1,0:T(8,128)(2,1)S(1)}, bf16[2,32,2048]{2,1,0:T(8,128)(2,1)S(1)}, u32[]{:S(2)}, u32[]{:S(2)}) collective-permute-start(bf16[2,32,2048]{2,1,0:T(8,128)(2,1)S(1)} %pad_maximum_fusion.3), channel_id=1, source_target_pairs={{0,2},{2,4},{4,6},{6,0},{1,3},{3,5},{5,7},{7,1},{8,10},{10,12},{12... | collective-permute-start | bytes 786440 | tf_op jit(solution)/shard_map/ppermute | solution.py:64
  129.0 21.1 %collective-permute-start.8 = (bf16[2,128,1024]{2,1,0:T(8,128)(2,1)S(1)}, bf16[2,128,1024]{2,1,0:T(8,128)(2,1)S(1)}, u32[]{:S(2)}, u32[]{:S(2)}) collective-permute-start(bf16[2,128,1024]{2,1,0:T(8,128)(2,1)S(1)} %collective-permute-done.7), channel_id=1, source_target_pairs={{0,2},{2,4},{4,6},{6,0},{1,3},{3,5},{5,7},{7,1},{8,10},{10,12},{12... | collective-permute-start | bytes 1572872 | tf_op jit(solution)/shard_map/ppermute | solution.py:64
  134.6 15.4 %collective-permute-start.14 = (bf16[2,32,2048]{2,1,0:T(8,128)(2,1)S(1)}, bf16[2,32,2048]{2,1,0:T(8,128)(2,1)S(1)}, u32[]{:S(2)}, u32[]{:S(2)}) collective-permute-start(bf16[2,32,2048]{2,1,0:T(8,128)(2,1)S(1)} %collective-permute-done.13), channel_id=1, source_target_pairs={{0,2},{2,4},{4,6},{6,0},{1,3},{3,5},{5,7},{7,1},{8,10},{10,12},{12... | collective-permute-start | bytes 786440 | tf_op jit(solution)/shard_map/ppermute | solution.py:64
  150.0 23.0 %collective-permute-start.15 = (bf16[2,32,2048]{2,1,0:T(8,128)(2,1)S(1)}, bf16[2,32,2048]{2,1,0:T(8,128)(2,1)S(1)}, u32[]{:S(2)}, u32[]{:S(2)}) collective-permute-start(bf16[2,32,2048]{2,1,0:T(8,128)(2,1)S(1)} %collective-permute-done.14), channel_id=1, source_target_pairs={{0,2},{2,4},{4,6},{6,0},{1,3},{3,5},{5,7},{7,1},{8,10},{10,12},{12... | collective-permute-start | bytes 786440 | tf_op jit(solution)/shard_map/ppermute | solution.py:64
  150.0 19.9 %collective-permute-start.9 = (bf16[2,128,1024]{2,1,0:T(8,128)(2,1)S(1)}, bf16[2,128,1024]{2,1,0:T(8,128)(2,1)S(1)}, u32[]{:S(2)}, u32[]{:S(2)}) collective-permute-start(bf16[2,128,1024]{2,1,0:T(8,128)(2,1)S(1)} %collective-permute-done.8), channel_id=1, source_target_pairs={{0,2},{2,4},{4,6},{6,0},{1,3},{3,5},{5,7},{7,1},{8,10},{10,12},{12... | collective-permute-start | bytes 1572872 | tf_op jit(solution)/shard_map/ppermute | solution.py:64
  171.1 72.4 %collective-permute-start.10 = (bf16[8,128,1024]{2,1,0:T(8,128)(2,1)}, bf16[8,128,1024]{2,1,0:T(8,128)(2,1)}, u32[]{:S(2)}, u32[]{:S(2)}) collective-permute-start(bf16[8,128,1024]{2,1,0:T(8,128)(2,1)} %get-tuple-element.66), channel_id=1, source_target_pairs={{0,16},{16,0},{1,17},{17,1},{2,18},{18,2},{3,19},{19,3},{4,20},{20... | collective-permute-start | bytes 6291464 | tf_op jit(solution)/shard_map/ppermute | solution.py:64
  173.8 65.2 %collective-permute-start.16 = (bf16[8,32,2048]{2,1,0:T(8,128)(2,1)S(1)}, bf16[8,32,2048]{2,1,0:T(8,128)(2,1)S(1)}, u32[]{:S(2)}, u32[]{:S(2)}) collective-permute-start(bf16[8,32,2048]{2,1,0:T(8,128)(2,1)S(1)} %get-tuple-element.87), channel_id=1, source_target_pairs={{0,16},{16,0},{1,17},{17,1},{2,18},{18,2},{3,19},{19,3},{4,20},{20... | collective-permute-start | bytes 3145736 | tf_op jit(solution)/shard_map/ppermute | solution.py:64
  240.1 14.6 %collective-permute-start.17 = (bf16[16,32,2048]{2,1,0:T(8,128)(2,1)}, bf16[16,32,2048]{2,1,0:T(8,128)(2,1)}, u32[]{:S(2)}, u32[]{:S(2)}) collective-permute-start(bf16[16,32,2048]{2,1,0:T(8,128)(2,1)} %constant_dynamic-update-slice_fusion.27.refs_0_), channel_id=1, source_target_pairs={{0,8},{8,0},{1,9},{9,1},{2,10},{10,2},{3,11},{11,3},{4,12},{12,4},... | collective-permute-start | bytes 6291464 | tf_op jit(solution)/shard_map/ppermute | solution.py:64
  246.6 49.7 %collective-permute-start.11 = (bf16[16,128,1024]{2,1,0:T(8,128)(2,1)}, bf16[16,128,1024]{2,1,0:T(8,128)(2,1)}, u32[]{:S(2)}, u32[]{:S(2)}) collective-permute-start(bf16[16,128,1024]{2,1,0:T(8,128)(2,1)} %constant_dynamic-update-slice_fusion.16.refs_3_), channel_id=1, source_target_pairs={{0,8},{8,0},{1,9},{9,1},{2,10},{10,2},{3,11},{11,3},{4,12},{12,4},... | collective-permute-start | bytes 12582920 | tf_op jit(solution)/shard_map/ppermute | solution.py:64
  481.1 89.5 %collective-permute-start.48 = (bf16[2,4,2,128,1024]{4,3,2,1,0:T(8,128)(2,1)}, bf16[2,4,2,128,1024]{4,3,2,1,0:T(8,128)(2,1)}, u32[]{:S(2)}, u32[]{:S(2)}) collective-permute-start(bf16[2,4,2,128,1024]{4,3,2,1,0:T(8,128)(2,1)} %bitcast.390), channel_id=1, source_target_pairs={{0,8},{8,0},{1,9},{9,1},{2,10},{10,2},{3,11},{11,3},{4,12},{12,4},... | collective-permute-start | bytes 12582920 | tf_op jit(solution)/shard_map/ppermute | solution.py:569
  481.1 93.7 %collective-permute-start.42 = (bf16[2,4,2,32,4096]{4,3,2,1,0:T(8,128)(2,1)}, bf16[2,4,2,32,4096]{4,3,2,1,0:T(8,128)(2,1)}, u32[]{:S(2)}, u32[]{:S(2)}) collective-permute-start(bf16[2,4,2,32,4096]{4,3,2,1,0:T(8,128)(2,1)} %bitcast.389), channel_id=1, source_target_pairs={{0,8},{8,0},{1,9},{9,1},{2,10},{10,2},{3,11},{11,3},{4,12},{12,4},... | collective-permute-start | bytes 12582920 | tf_op jit(solution)/shard_map/ppermute | solution.py:569
  486.7 34.5 %collective-permute-start.36 = (bf16[2,4,2,32,1024]{4,3,2,1,0:T(8,128)(2,1)}, bf16[2,4,2,32,1024]{4,3,2,1,0:T(8,128)(2,1)S(1)}, u32[]{:S(2)}, u32[]{:S(2)}) collective-permute-start(bf16[2,4,2,32,1024]{4,3,2,1,0:T(8,128)(2,1)} %bitcast.382), channel_id=1, source_target_pairs={{0,8},{8,0},{1,9},{9,1},{2,10},{10,2},{3,11},{11,3},{4,12},{12,4},... | collective-permute-start | bytes 3145736 | tf_op jit(solution)/shard_map/ppermute | solution.py:569
  486.7 61.4 %collective-permute-start.24 = (bf16[2,4,2,32,1536]{4,3,2,1,0:T(8,128)(2,1)}, bf16[2,4,2,32,1536]{4,3,2,1,0:T(8,128)(2,1)}, u32[]{:S(2)}, u32[]{:S(2)}) collective-permute-start(bf16[2,4,2,32,1536]{4,3,2,1,0:T(8,128)(2,1)} %bitcast.79), channel_id=1, source_target_pairs={{0,8},{8,0},{1,9},{9,1},{2,10},{10,2},{3,11},{11,3},{4,12},{12,4},... | collective-permute-start | bytes 4718600 | tf_op jit(solution)/shard_map/ppermute | solution.py:569
  534.5 29.9 %collective-permute-start.30 = (bf16[2,4,2,32,1536]{4,3,2,1,0:T(8,128)(2,1)}, bf16[2,4,2,32,1536]{4,3,2,1,0:T(8,128)(2,1)S(1)}, u32[]{:S(2)}, u32[]{:S(2)}) collective-permute-start(bf16[2,4,2,32,1536]{4,3,2,1,0:T(8,128)(2,1)} %bitcast.378), channel_id=1, source_target_pairs={{0,8},{8,0},{1,9},{9,1},{2,10},{10,2},{3,11},{11,3},{4,12},{12,4},... | collective-permute-start | bytes 4718600 | tf_op jit(solution)/shard_map/ppermute | solution.py:569
  549.5 20.0 %collective-permute-start.25 = (bf16[2,4,32,1536]{3,2,1,0:T(8,128)(2,1)S(1)}, bf16[2,4,32,1536]{3,2,1,0:T(8,128)(2,1)S(1)}, u32[]{:S(2)}, u32[]{:S(2)}) collective-permute-start(bf16[2,4,32,1536]{3,2,1,0:T(8,128)(2,1)S(1)} %fusion.12), channel_id=1, source_target_pairs={{0,1},{1,0},{2,3},{3,2},{4,5},{5,4},{6,7},{7,6},{8,9},{9,8},{10,11... | collective-permute-start | bytes 2359304 | tf_op jit(solution)/shard_map/ppermute | solution.py:127
  564.6 20.5 %collective-permute-start.31 = (bf16[4,2,32,1536]{3,2,1,0:T(8,128)(2,1)S(1)}, bf16[4,2,32,1536]{3,2,1,0:T(8,128)(2,1)S(1)}, u32[]{:S(2)}, u32[]{:S(2)}) collective-permute-start(bf16[4,2,32,1536]{3,2,1,0:T(8,128)(2,1)S(1)} %fusion.13), channel_id=1, source_target_pairs={{0,16},{16,0},{1,17},{17,1},{2,18},{18,2},{3,19},{19,3},{4,20},{20... | collective-permute-start | bytes 2359304 | tf_op jit(solution)/shard_map/ppermute | solution.py:127
  570.5 14.8 %collective-permute-start.26 = (bf16[2,32,1536]{2,1,0:T(8,128)(2,1)S(1)}, bf16[2,32,1536]{2,1,0:T(8,128)(2,1)S(1)}, u32[]{:S(2)}, u32[]{:S(2)}) collective-permute-start(bf16[2,32,1536]{2,1,0:T(8,128)(2,1)S(1)} %fusion.24), channel_id=1, source_target_pairs={{0,2},{2,4},{4,6},{6,0},{1,3},{3,5},{5,7},{7,1},{8,10},{10,12},{12... | collective-permute-start | bytes 589832 | tf_op jit(solution)/shard_map/ppermute | solution.py:127
  573.3 40.7 %collective-permute-start.49 = (bf16[2,4,128,1024]{3,2,1,0:T(8,128)(2,1)S(1)}, bf16[2,4,128,1024]{3,2,1,0:T(8,128)(2,1)S(1)}, u32[]{:S(2)}, u32[]{:S(2)}) collective-permute-start(bf16[2,4,128,1024]{3,2,1,0:T(8,128)(2,1)S(1)} %fusion.1), channel_id=1, source_target_pairs={{0,1},{1,0},{2,3},{3,2},{4,5},{5,4},{6,7},{7,6},{8,9},{9,8},{10,11... | collective-permute-start | bytes 6291464 | tf_op jit(solution)/shard_map/ppermute | solution.py:127
  577.1 47.9 %collective-permute-start.43 = (bf16[4,2,32,4096]{3,2,1,0:T(8,128)(2,1)S(1)}, bf16[4,2,32,4096]{3,2,1,0:T(8,128)(2,1)S(1)}, u32[]{:S(2)}, u32[]{:S(2)}) collective-permute-start(bf16[4,2,32,4096]{3,2,1,0:T(8,128)(2,1)S(1)} %fusion), channel_id=1, source_target_pairs={{0,16},{16,0},{1,17},{17,1},{2,18},{18,2},{3,19},{19,3},{4,20},{20... | collective-permute-start | bytes 6291464 | tf_op jit(solution)/shard_map/ppermute | solution.py:127
  598.0 28.3 %collective-permute-start.28 = (bf16[2,32,1536]{2,1,0:T(8,128)(2,1)S(1)}, bf16[2,32,1536]{2,1,0:T(8,128)(2,1)S(1)}, u32[]{:S(2)}, u32[]{:S(2)}) collective-permute-start(bf16[2,32,1536]{2,1,0:T(8,128)(2,1)S(1)} %fusion.28), channel_id=1, source_target_pairs={{0,2},{2,4},{4,6},{6,0},{1,3},{3,5},{5,7},{7,1},{8,10},{10,12},{12... | collective-permute-start | bytes 589832 | tf_op jit(solution)/shard_map/ppermute | solution.py:127
  602.3 26.1 %collective-permute-start.34 = (bf16[2,32,1536]{2,1,0:T(8,128)(2,1)S(1)}, bf16[2,32,1536]{2,1,0:T(8,128)(2,1)S(1)}, u32[]{:S(2)}, u32[]{:S(2)}) collective-permute-start(bf16[2,32,1536]{2,1,0:T(8,128)(2,1)S(1)} %fusion.23), channel_id=1, source_target_pairs={{0,2},{2,4},{4,6},{6,0},{1,3},{3,5},{5,7},{7,1},{8,10},{10,12},{12... | collective-permute-start | bytes 589832 | tf_op jit(solution)/shard_map/ppermute | solution.py:127
  626.2 16.7 %collective-permute-start.44 = (bf16[2,32,4096]{2,1,0:T(8,128)(2,1)S(1)}, bf16[2,32,4096]{2,1,0:T(8,128)(2,1)S(1)}, u32[]{:S(2)}, u32[]{:S(2)}) collective-permute-start(bf16[2,32,4096]{2,1,0:T(8,128)(2,1)S(1)} %fusion.7), channel_id=1, source_target_pairs={{0,2},{2,4},{4,6},{6,0},{1,3},{3,5},{5,7},{7,1},{8,10},{10,12},{12... | collective-permute-start | bytes 1572872 | tf_op jit(solution)/shard_map/ppermute | solution.py:127
  627.3 17.0 %collective-permute-start.29 = (bf16[32,1536]{1,0:T(8,128)(2,1)S(1)}, bf16[32,1536]{1,0:T(8,128)(2,1)S(1)}, u32[]{:S(2)}, u32[]{:S(2)}) collective-permute-start(bf16[32,1536]{1,0:T(8,128)(2,1)S(1)} %fusion.39), channel_id=1, source_target_pairs={{0,16},{16,0},{1,17},{17,1},{2,18},{18,2},{3,19},{19,3},{4,20},{20... | collective-permute-start | bytes 294920 | tf_op jit(solution)/shard_map/ppermute | solution.py:127
  628.4 38.4 %collective-permute-start.35 = (bf16[32,1536]{1,0:T(8,128)(2,1)S(1)}, bf16[32,1536]{1,0:T(8,128)(2,1)S(1)}, u32[]{:S(2)}, u32[]{:S(2)}) collective-permute-start(bf16[32,1536]{1,0:T(8,128)(2,1)S(1)} %fusion.37), channel_id=1, source_target_pairs={{0,1},{1,0},{2,3},{3,2},{4,5},{5,4},{6,7},{7,6},{8,9},{9,8},{10,11... | collective-permute-start | bytes 294920 | tf_op jit(solution)/shard_map/ppermute | solution.py:127
  630.7 23.4 %collective-permute-start.51 = (bf16[2,128,1024]{2,1,0:T(8,128)(2,1)S(1)}, bf16[2,128,1024]{2,1,0:T(8,128)(2,1)S(1)}, u32[]{:S(2)}, u32[]{:S(2)}) collective-permute-start(bf16[2,128,1024]{2,1,0:T(8,128)(2,1)S(1)} %fusion.4), channel_id=1, source_target_pairs={{0,2},{2,4},{4,6},{6,0},{1,3},{3,5},{5,7},{7,1},{8,10},{10,12},{12... | collective-permute-start | bytes 1572872 | tf_op jit(solution)/shard_map/ppermute | solution.py:127
  644.2 21.2 %collective-permute-start.45 = (bf16[2,32,4096]{2,1,0:T(8,128)(2,1)S(1)}, bf16[2,32,4096]{2,1,0:T(8,128)(2,1)S(1)}, u32[]{:S(2)}, u32[]{:S(2)}) collective-permute-start(bf16[2,32,4096]{2,1,0:T(8,128)(2,1)S(1)} %fusion.9), channel_id=1, source_target_pairs={{0,2},{2,4},{4,6},{6,0},{1,3},{3,5},{5,7},{7,1},{8,10},{10,12},{12... | collective-permute-start | bytes 1572872 | tf_op jit(solution)/shard_map/ppermute | solution.py:127
  655.6 21.1 %collective-permute-start.52 = (bf16[2,128,1024]{2,1,0:T(8,128)(2,1)S(1)}, bf16[2,128,1024]{2,1,0:T(8,128)(2,1)S(1)}, u32[]{:S(2)}, u32[]{:S(2)}) collective-permute-start(bf16[2,128,1024]{2,1,0:T(8,128)(2,1)S(1)} %fusion.6), channel_id=1, source_target_pairs={{0,2},{2,4},{4,6},{6,0},{1,3},{3,5},{5,7},{7,1},{8,10},{10,12},{12... | collective-permute-start | bytes 1572872 | tf_op jit(solution)/shard_map/ppermute | solution.py:127
  666.7 15.9 %collective-permute-start.46 = (bf16[2,32,4096]{2,1,0:T(8,128)(2,1)S(1)}, bf16[2,32,4096]{2,1,0:T(8,128)(2,1)S(1)}, u32[]{:S(2)}, u32[]{:S(2)}) collective-permute-start(bf16[2,32,4096]{2,1,0:T(8,128)(2,1)S(1)} %fusion.11), channel_id=1, source_target_pairs={{0,2},{2,4},{4,6},{6,0},{1,3},{3,5},{5,7},{7,1},{8,10},{10,12},{12... | collective-permute-start | bytes 1572872 | tf_op jit(solution)/shard_map/ppermute | solution.py:127
  (38 other events, 712.0 us)
Sparse Core Ops, SparseCore 0:
  11.0 97.7 all-gather.1
